TPU v7x, 128 devices: a whole 4x4x4 slice. The times are simulated.
128 devices in a mesh: seq: 32 (over z, x_lo, y), head: 4 (over x_hi, core).
Axes of the slice: x: 4 (x_hi: 2, x_lo: 2; x = x_hi * 2 + x_lo), y: 4, z: 4, core: 2. Of those that a mesh axis runs over, the one named last changes fastest.
Arguments:
- hidden_in: bfloat16 [12, 2048, 1024], P(None, 'seq'), may hold values from -48 to 48
- lengths: int32 [12], replicated, may hold values from 1 to 2048, as said below
- w_qkv: float32 [1024, 3072], P(('seq', 'head')), may hold values from -0.1875 to 0.1875
- w_attn_out: float32 [1024, 1024], P(('seq', 'head')), may hold values from -0.1875 to 0.1875
- w_in: float32 [1024, 4096], P(('seq', 'head')), may hold values from -0.1875 to 0.1875
- w_down: float32 [4096, 1024], P(('seq', 'head')), may hold values from -0.09375 to 0.09375
- ln_gain: float32 [2, 1024], replicated, may hold values from 0.5 to 1.5
- ln_bias: float32 [2, 1024], replicated, may hold values from -1.5 to 1.5
Outputs:
- hidden_out: bfloat16 [12, 2048, 1024], P(None, 'seq', 'head')
- key_cache: bfloat16 [12, 2048, 1024], P(None, 'seq', 'head')
- value_cache: bfloat16 [12, 2048, 1024], P(None, 'seq', 'head')
Inputs may be any that keep to these rules, and one draw needn't show every extreme that they name: `lengths`: the longest prompt has exactly 2048 positions.
All inputs are finite; a program needn't handle non-finite values.
Results may differ from a plain program's by a relative error of at most 0.014.
Values may be sent and summed in bfloat16 or wider, within the bound.
A program may use at most 192 MiB of HBM per device.

v0:
```python
import jax
import jax.numpy as jnp
from jax import lax
from jax.sharding import PartitionSpec as P

D = 1024
HEADS = 16
HEAD_DIM = 64


EPSILON = 1e-05


def layer_norm(row_values, gain_row, shift_row):
    row_sums, squares = lax.psum(
        (jnp.sum(row_values, axis=1), jnp.sum(row_values * row_values, axis=1)), "head"
    )
    average = (row_sums / D)[:, None]
    spread = (squares / D)[:, None] - average * average
    return (row_values - average) * lax.rsqrt(spread + EPSILON) * gain_row + shift_row


def relayout(qkv_stripe, out_stripe, in_stripe, group_count, seq_count):
    gathered = (
        lax.all_gather(qkv_stripe, "seq", axis=0, tiled=True),
        lax.all_gather(out_stripe, "seq", axis=0, tiled=True),
        lax.all_gather(in_stripe, "seq", axis=0, tiled=True),
    )
    exchanged = (
        lax.all_to_all(gathered[0], "head", split_axis=1, concat_axis=0, tiled=True),
        lax.all_to_all(gathered[1], "head", split_axis=1, concat_axis=0, tiled=True),
        lax.all_to_all(gathered[2], "head", split_axis=1, concat_axis=0, tiled=True),
    )
    result = []
    for piece in exchanged:
        columns = piece.shape[2]
        reordered = piece.reshape(group_count, seq_count, -1, columns).transpose(1, 0, 2, 3)
        result.append(reordered.reshape(-1, columns))
    return tuple(result)


def per_device(hidden_in, lengths, w_qkv, w_attn_out, w_in, w_down, ln_gain, ln_bias):
    group_count = lax.axis_size("head")
    seq_count = lax.axis_size("seq")
    head_group = lax.axis_index("head")
    seq_block = lax.axis_index("seq")
    local_rows = w_qkv.shape[0]
    unit_rows = w_down.shape[0]
    group_width = D // group_count
    heads_here = HEADS // group_count
    prompt_count = hidden_in.shape[0]
    local_span = hidden_in.shape[1]
    qkv_stripe = w_qkv.astype(jnp.bfloat16).reshape(local_rows, 3, group_count, group_width)
    qkv_stripe = qkv_stripe.transpose(0, 2, 1, 3).reshape(local_rows, group_count, 3 * group_width)
    out_stripe = w_attn_out.astype(jnp.bfloat16).reshape(local_rows, group_count, group_width)
    in_stripe = w_in.astype(jnp.bfloat16).reshape(local_rows, seq_count, group_count, unit_rows)
    in_stripe = in_stripe.transpose(0, 2, 1, 3).reshape(
        local_rows, group_count, seq_count * unit_rows
    )
    qkv_weight, out_weight, in_weight = relayout(
        qkv_stripe, out_stripe, in_stripe, group_count, seq_count
    )
    token_rows = hidden_in.reshape(prompt_count * local_span, D)
    projected = jnp.dot(token_rows, qkv_weight, preferred_element_type=jnp.float32).astype(
        jnp.bfloat16
    )
    projected = projected.reshape(prompt_count, local_span, 3, heads_here, HEAD_DIM)
    positions = seq_block * local_span + jnp.arange(local_span, dtype=jnp.int32)
    live_mask = positions[None, :] < lengths[:, None]
    zero_value = jnp.zeros((), jnp.bfloat16)
    queries = projected[:, :, 0]
    keys_here = jnp.where(live_mask[:, :, None, None], projected[:, :, 1], zero_value)
    values_here = jnp.where(live_mask[:, :, None, None], projected[:, :, 2], zero_value)
    keys_all, values_all = (
        lax.all_gather(keys_here, "seq", axis=1, tiled=True),
        lax.all_gather(values_here, "seq", axis=1, tiled=True),
    )
    key_live = jnp.arange(keys_all.shape[1], dtype=jnp.int32)[None, :] < lengths[:, None]
    score_scale = HEAD_DIM ** (-0.5)

    def one_prompt(prompt_items):
        query_rows, key_rows, value_rows, live_keys = prompt_items
        scores = (
            jnp.einsum("qhd,khd->hqk", query_rows, key_rows, preferred_element_type=jnp.float32)
            * score_scale
        )
        scores = jnp.where(live_keys[None, None, :], scores, -jnp.inf)
        row_max = jnp.max(scores, axis=-1, keepdims=True)
        exp_terms = jnp.exp(scores - row_max)
        soft_weights = (exp_terms / jnp.sum(exp_terms, axis=-1, keepdims=True)).astype(jnp.bfloat16)
        head_mix = jnp.einsum(
            "hqk,khd->qhd", soft_weights, value_rows, preferred_element_type=jnp.float32
        )
        return head_mix.astype(jnp.bfloat16)

    attended = lax.map(one_prompt, (queries, keys_all, values_all, key_live))
    attended = attended.reshape(prompt_count * local_span, group_width)
    joined = lax.all_gather(attended, "head", axis=1, tiled=True)
    start = head_group * group_width
    own_columns = lax.dynamic_slice_in_dim(token_rows, start, group_width, 1).astype(jnp.float32)
    gain_first = lax.dynamic_slice_in_dim(ln_gain[0], start, group_width, 0)
    shift_first = lax.dynamic_slice_in_dim(ln_bias[0], start, group_width, 0)
    gain_second = lax.dynamic_slice_in_dim(ln_gain[1], start, group_width, 0)
    shift_second = lax.dynamic_slice_in_dim(ln_bias[1], start, group_width, 0)
    attn_sum = jnp.dot(joined, out_weight, preferred_element_type=jnp.float32) + own_columns
    normed = layer_norm(attn_sum, gain_first, shift_first).astype(jnp.bfloat16)
    normed_all = lax.all_gather(normed, "head", axis=1, tiled=True)
    hidden_units = jax.nn.gelu(
        jnp.dot(normed_all, in_weight, preferred_element_type=jnp.float32), approximate=False
    ).astype(jnp.bfloat16)
    down_weight = lax.all_gather(w_down.astype(jnp.bfloat16), "seq", axis=0, tiled=True)
    partial_terms = jnp.dot(hidden_units, down_weight, preferred_element_type=jnp.float32)
    down_part = lax.psum_scatter(
        partial_terms.astype(jnp.bfloat16), "head", scatter_dimension=1, tiled=True
    ).astype(jnp.float32)
    ffn_sum = down_part + normed.astype(jnp.float32)
    hidden_out = layer_norm(ffn_sum, gain_second, shift_second).astype(jnp.bfloat16)
    hidden_out = hidden_out.reshape(prompt_count, local_span, group_width)
    key_cache = keys_here.reshape(prompt_count, local_span, group_width)
    value_cache = values_here.reshape(prompt_count, local_span, group_width)
    return (hidden_out, key_cache, value_cache)


def solution(mesh):
    in_specs = (
        P(None, "seq", None),
        P(),
        P(("seq", "head"), None),
        P(("seq", "head"), None),
        P(("seq", "head"), None),
        P(("seq", "head"), None),
        P(),
        P(),
    )
    out_specs = (P(None, "seq", "head"), P(None, "seq", "head"), P(None, "seq", "head"))
    return jax.shard_map(
        per_device, mesh=mesh, in_specs=in_specs, out_specs=out_specs, check_vma=False
    )
```

profile of v0, /device:TPU:1, one launch (start us, length us, event | category | flops | bytes accessed | tf_op | source)
XLA Modules:
  0.0 1285.0 jit_solution(5143140646698447728)
XLA Ops:
  7.2 0.9 convert_element_type.45
  8.2 0.7 reshape.116
  8.9 136.6 %all-gather.8.cloned.1.call-done = bf16[256,4,768]{2,0,1:T(8,128)(2,1)} async-done(((bf16[8,4,768]{2,0,1:T(8,128)(2,1)}), bf16[256,4,768]{2,0,1:T(8,128)(2,1)}) %all-gather.8.cloned.1.call-update) | async-done | bytes 1572880 | tf_op jit(solution)/shard_map/all_gather | solution.py:25
  145.4 25.0 %all-to-all-start = ((bf16[256,4,768]{2,0,1:T(8,128)(2,1)}), bf16[256,4,768]{2,0,1:T(8,128)(2,1)S(1)}, u32[]{:S(2)}, u32[]{:S(2)}) async-start(bf16[256,4,768]{2,0,1:T(8,128)(2,1)} %all-gather.8.cloned.1.call-done), calls=%async_computation | async-start | bytes 3145728 | tf_op jit(solution)/shard_map/all_to_all | solution.py:30
  170.7 20.5 %all-to-all-done = bf16[256,4,768]{2,0,1:T(8,128)(2,1)S(1)} async-done(((bf16[256,4,768]{2,0,1:T(8,128)(2,1)}), bf16[256,4,768]{2,0,1:T(8,128)(2,1)S(1)}, u32[]{:S(2)}, u32[]{:S(2)}) %all-to-all-start) | async-done | bytes 1572896 | tf_op jit(solution)/shard_map/all_to_all | solution.py:30
  191.4 2.8 convolution_convert_fusion.2
  194.2 1.3 reshape.119
  195.6 1.8 fusion.105
  197.4 0.9 copy-done
  198.2 2.4 bitcast_select_fusion
  200.8 0.7 all-gather.12.cloned.1.call-update
  201.8 275.5 %all-gather.10.cloned.1.call-done = bf16[12,2048,4,64]{3,2,0,1:T(4,128)(2,1)} async-done(((bf16[12,64,4,64]{3,2,0,1:T(4,128)(2,1)}), bf16[12,2048,4,64]{3,2,0,1:T(4,128)(2,1)}) %all-gather.10.cloned.1.call-update) | async-done | bytes 12582928 | tf_op jit(solution)/shard_map/all_gather | solution.py:76
  477.3 35.9 %copy.59 = bf16[12,2048,4,64]{1,3,2,0:T(8,128)(2,1)} copy(bf16[12,2048,4,64]{3,2,0,1:T(4,128)(2,1)} %all-gather.10.cloned.1.call-done) | data formatting | bytes 25165824 | tf_op jit(solution)/shard_map/while | solution.py:96
  513.2 240.0 %all-gather.12.cloned.1.call-done = bf16[12,2048,4,64]{3,2,0,1:T(4,128)(2,1)} async-done(((bf16[12,64,4,64]{3,2,0,1:T(4,128)(2,1)}), bf16[12,2048,4,64]{3,2,0,1:T(4,128)(2,1)}) %all-gather.12.cloned.1.call-update) | async-done | bytes 12582928 | tf_op jit(solution)/shard_map/all_gather | solution.py:75
  753.2 35.9 %copy.60 = bf16[12,2048,4,64]{1,3,2,0:T(8,128)(2,1)} copy(bf16[12,2048,4,64]{3,2,0,1:T(4,128)(2,1)} %all-gather.12.cloned.1.call-done) | data formatting | bytes 25165824 | tf_op jit(solution)/shard_map/while | solution.py:96
  789.1 71.2 %while.10 = (s32[]{:T(128)}, bf16[12,64,4,64]{3,2,1,0:T(4,128)(2,1)S(1)}, bf16[12,2048,4,64]{1,3,2,0:T(8,128)(2,1)}, pred[12,2048]{1,0:T(8,128)(4,1)S(1)}, bf16[...) while((s32[]{:T(128)}, bf16[12,64,4,64]{3,2,1,0:T(4,128)(2,1)S(1)}, ...), condition=%wide.region_3.4_spmd, body=%wide.region_0.3_spmd.sunk | while | flops 137381888 | bytes 6596181 | solution.py:96
  789.1 3.3 fusion.125
  792.5 2.4 fusion.126
  795.1 3.3 fusion.125
  798.4 2.4 fusion.126
  801.0 3.3 fusion.125
  804.3 2.4 fusion.126
  807.0 3.3 fusion.125
  810.2 2.4 fusion.126
  812.9 3.3 fusion.125
  816.2 2.4 fusion.126
  818.8 3.3 fusion.125
  822.1 2.4 fusion.126
  824.8 3.3 fusion.125
  828.0 2.4 fusion.126
  830.7 3.3 fusion.125
  834.0 2.4 fusion.126
  836.6 3.3 fusion.125
  839.9 2.4 fusion.126
  842.5 3.3 fusion.125
  845.8 2.4 fusion.126
  848.5 3.3 fusion.125
  851.7 2.4 fusion.126
  854.4 3.3 fusion.125
  857.7 2.4 fusion.126
  860.3 1.2 reshape.120
  861.9 0.9 reshape.125
  862.9 0.6 convert_element_type.52
  863.6 71.0 %all_gather.28 = bf16[256,4,256]{2,0,1:T(8,128)(2,1)} all-gather(bf16[8,4,256]{2,0,1:T(8,128)(2,1)S(1)} %bitcast.105), channel_id=1, replica_groups=mesh['seq'=32,'head'=4] {'seq'}, dimensions={0}, use_global_device_ids=true | all-gather | bytes 540672 | tf_op jit(solution)/shard_map/all_gather | solution.py:26
  934.6 18.0 %all-to-all-start.1 = ((bf16[256,4,256]{2,0,1:T(8,128)(2,1)}), bf16[256,4,256]{2,0,1:T(8,128)(2,1)S(1)}, u32[]{:S(2)}, u32[]{:S(2)}) async-start(bf16[256,4,256]{2,0,1:T(8,128)(2,1)} %all_gather.28), calls=%async_computation.1 | async-start | bytes 1048576 | tf_op jit(solution)/shard_map/all_to_all | solution.py:31
  952.7 10.4 all-to-all-done.1
  963.2 2.2 fusion.99
  965.3 7.4 all-reduce.1
  972.7 1.0 add_convert_fusion.1
  973.8 43.7 %all-gather.18.cloned.1.call-done = bf16[256,4,1024]{2,0,1:T(8,128)(2,1)} async-done(((bf16[8,4,1024]{2,0,1:T(8,128)(2,1)}), bf16[256,4,1024]{2,0,1:T(8,128)(2,1)}) %all-gather.18.cloned.1.call-update) | async-done | bytes 2097168 | tf_op jit(solution)/shard_map/all_gather | solution.py:27
  1017.6 54.6 %all_to_all.45 = bf16[256,4,1024]{2,0,1:T(8,128)(2,1)S(1)} all-to-all(bf16[256,4,1024]{2,0,1:T(8,128)(2,1)} %all-gather.18.cloned.1.call-done), channel_id=1, replica_groups=mesh['seq'=32,'head'=4] {'head'}, dimensions={1} | all-to-all | bytes 4194304 | tf_op jit(solution)/shard_map/all_to_all | solution.py:32
  1072.2 1.5 copy.64
  1073.6 100.2 %all-gather.20.cloned.1.call-done = bf16[1024,1024]{1,0:T(8,128)(2,1)} async-done(((bf16[32,1024]{1,0:T(8,128)(2,1)}), bf16[1024,1024]{1,0:T(8,128)(2,1)}) %all-gather.20.cloned.1.call-update) | async-done | bytes 2097168 | tf_op jit(solution)/shard_map/all_gather | solution.py:111
  1173.8 45.7 %all-gather.16.cloned.1.call-done = bf16[768,1024]{1,0:T(8,128)(2,1)} async-done(((bf16[768,256]{1,0:T(8,128)(2,1)}), bf16[768,1024]{1,0:T(8,128)(2,1)}) %all-gather.16.cloned.1.call-update) | async-done | bytes 1572880 | tf_op jit(solution)/shard_map/all_gather | solution.py:107
  1219.6 13.3 %convolution_convert_fusion.1 = bf16[768,1024]{1,0:T(8,128)(2,1)} fusion(bf16[1024,1024]{1,0:T(8,128)(2,1)} %all-gather.20.cloned.1.call-done, bf16[768,1024]{1,0:T(8,128)(2,1)} %all-gather.16.cloned.1.call-done, bf16[1024,1024]{1,0:T(8,128)(2,1)} %bitcast.96), kind=kOutput, calls=%fused_computation.43 | convolution fusion | flops 3273129984 | bytes 7340032 | tf_op jit(solution)/shard_map/dot_general | solution.py:112
  1232.9 0.5 reshape.132
  1233.4 0.5 reshape.133
  1233.9 0.2 copy.81
  1234.1 0.2 copy.82
  1234.3 1.2 copy_select_fusion
  1235.5 31.7 %reduce-scatter.2.cloned.1.call-done = bf16[768,256]{1,0:T(8,128)(2,1)} async-done(((bf16[768,1024]{1,0:T(8,128)(2,1)}), bf16[768,256]{1,0:T(8,128)(2,1)}) %reduce-scatter.2.cloned.1.call-update) | async-done | bytes 393232 | tf_op jit(solution)/shard_map/reduce_scatter | solution.py:113
  1267.1 1.5 fusion.68
  1268.6 7.3 all-reduce
  1276.0 2.2 add_convert_fusion
  (88 shorter events, 3.8 us)
Async XLA Ops:
  7.2 163.3 %copy-start.8 = (s32[12]{0:T(128)S(1)}, s32[12]{0:T(128)}, u32[]{:S(2)}) copy-start(s32[12]{0:T(128)} %param.11) | copy-start | bytes 148
  7.2 138.3 %all-gather.8.cloned.1.call-start = ((), (), s32[]{:S(2)}) async-start(), calls=%async_computation.4 | async-start | bytes 1622016 | tf_op jit(solution)/shard_map/all_gather | solution.py:25
  145.4 45.8 %all-to-all-start = ((bf16[256,4,768]{2,0,1:T(8,128)(2,1)}), bf16[256,4,768]{2,0,1:T(8,128)(2,1)S(1)}, u32[]{:S(2)}, u32[]{:S(2)}) async-start(bf16[256,4,768]{2,0,1:T(8,128)(2,1)} %all-gather.8.cloned.1.call-done), calls=%async_computation | async-start | bytes 3145728 | tf_op jit(solution)/shard_map/all_to_all | solution.py:30
  170.5 306.8 %all-gather.10.cloned.1.call-start = ((), (), s32[]{:S(2)}) async-start(), calls=%async_computation.5 | async-start | bytes 25952256 | tf_op jit(solution)/shard_map/all_gather | solution.py:76
  197.4 0.9 copy-start
  197.4 4.2 copy-start.2
  200.7 552.5 %all-gather.12.cloned.1.call-start = ((), (), s32[]{:S(2)}) async-start(), calls=%async_computation.6 | async-start | bytes 25952256 | tf_op jit(solution)/shard_map/all_gather | solution.py:75
  201.4 761.7 %all-gather.14.cloned.1.call-start = ((), (), s32[]{:S(2)}) async-start(), calls=%async_computation.7 | async-start | bytes 1966080 | tf_op jit(solution)/shard_map/all_gather | solution.py:98
  789.1 72.5 %copy-start.3 = (f32[8,4096]{1,0:T(8,128)S(1)}, f32[8,4096]{1,0:T(8,128)}, u32[]{:S(2)}) copy-start(f32[8,4096]{1,0:T(8,128)} %param.14) | copy-start | bytes 393220
  789.1 73.8 %copy-start.4 = (f32[32,1024]{1,0:T(8,128)S(1)}, f32[32,1024]{1,0:T(8,128)}, u32[]{:S(2)}) copy-start(f32[32,1024]{1,0:T(8,128)} %param.15) | copy-start | bytes 393220
  860.3 3.3 copy-start.5
  860.3 92.3 %copy-start.6 = (f32[2,1024]{1,0:T(2,128)S(1)}, f32[2,1024]{1,0:T(2,128)}, u32[]{:S(2)}) copy-start(f32[2,1024]{1,0:T(2,128)} %param.16) | copy-start | bytes 24580
  860.3 92.3 %copy-start.7 = (f32[2,1024]{1,0:T(2,128)S(1)}, f32[2,1024]{1,0:T(2,128)}, u32[]{:S(2)}) copy-start(f32[2,1024]{1,0:T(2,128)} %param.17) | copy-start | bytes 24580
  861.6 156.0 %all-gather.18.cloned.1.call-start = ((), (), s32[]{:S(2)}) async-start(), calls=%async_computation.9 | async-start | bytes 2162688 | tf_op jit(solution)/shard_map/all_gather | solution.py:27
  862.8 311.0 %all-gather.20.cloned.1.call-start = ((), (), s32[]{:S(2)}) async-start(), calls=%async_computation.10 | async-start | bytes 2162688 | tf_op jit(solution)/shard_map/all_gather | solution.py:111
  934.6 28.5 %all-to-all-start.1 = ((bf16[256,4,256]{2,0,1:T(8,128)(2,1)}), bf16[256,4,256]{2,0,1:T(8,128)(2,1)S(1)}, u32[]{:S(2)}, u32[]{:S(2)}) async-start(bf16[256,4,256]{2,0,1:T(8,128)(2,1)} %all_gather.28), calls=%async_computation.1 | async-start | bytes 1048576 | tf_op jit(solution)/shard_map/all_to_all | solution.py:31
  952.6 267.0 %all-gather.16.cloned.1.call-start = ((), (), s32[]{:S(2)}) async-start(), calls=%async_computation.8 | async-start | bytes 1966080 | tf_op jit(solution)/shard_map/all_gather | solution.py:107
  973.8 293.4 %reduce-scatter.2.cloned.1.call-start = ((), (), s32[]{:S(2)}) async-start(), calls=%async_computation.11 | async-start | bytes 1966080 | tf_op jit(solution)/shard_map/reduce_scatter | solution.py:113
  1219.6 13.3 %copy-start.1 = (bf16[12,64,1,4,64]{4,3,2,1,0:T(4,128)(2,1)S(1)}, bf16[12,64,1,4,64]{4,3,2,1,0:T(4,128)(2,1)}, u32[]{:S(2)}) copy-start(bf16[12,64,1,4,64]{4,3,2,1,0:T(4,128)(2,1)} %copy-done) | copy-start | bytes 1179652
Sparse Core Ops, SparseCore 0:
  10.2 135.1 all-gather.7
  200.8 276.4 all-gather.9
  478.9 274.2 all-gather.11
  861.7 21.3 all-gather.13
  885.2 132.3 all-gather.17
  1019.7 154.1 all-gather.19
  1176.1 43.4 all-gather.15
  1233.0 34.1 reduce-scatter.1
where the time goes:
time: 1290 us
  waiting for transfers between devices  905 us (70%)
  blocking collectives  140 us (11%)
  matrix products  86.7 us (7%)
  local copies, waits for them, and re-layouts  84.7 us (7%)
  starting transfers between devices  43.3 us (3%)
  between operations  14.4 us (1%)
    all_gather x1, waiting for transfers between devices, per_device(): lax.all_gather(values_here, 'seq', axis=1, tiled=True)  275 us
    all_gather x1, waiting for transfers between devices, per_device(): lax.all_gather(keys_here, 'seq', axis=1, tiled=True)  240 us
    all_gather x1, waiting for transfers between devices, relayout(): lax.all_gather(qkv_stripe, 'seq', axis=0, tiled=True)  137 us
    all_gather x1, waiting for transfers between devices, per_device(): lax.all_gather(w_down.astype(jnp.bfloat16), 'seq', axis=0, tiled=True)  100 us
    while x2, local copies, waits for them, and re-layouts, per_device(): attended = lax.map(one_prompt, (queries, keys_all, values_all, key_live))  71.8 us
    all_gather x1, blocking collectives, relayout(): lax.all_gather(out_stripe, 'seq', axis=0, tiled=True)  71 us
    all_to_all x1, blocking collectives, relayout(): lax.all_to_all(gathered[2], 'head', split_axis=1, concat_axis=0, tiled=True)  54.6 us
    all_gather x1, waiting for transfers between devices, per_device(): normed_all = lax.all_gather(normed, 'head', axis=1, tiled=True)  45.7 us
  transfers between devices with their start and end apart: 10, of which 9 were waited for; matrix products, arithmetic and copies ran while one was open for 4% of the time, Pallas kernels for 0%

commit v1 on v0

v1 whole, which is shorter than its diff:
```python
import functools
import math

import jax
import jax.numpy as jnp
from jax import lax
from jax.experimental import pallas as pl
from jax.experimental.pallas import tpu as pltpu
from jax.sharding import PartitionSpec as P

MESH = pl.DeviceIdType.MESH
BF = jnp.bfloat16
F32 = jnp.float32
EPSILON = 1e-05
SCORE_FACTOR = 64 ** (-0.5) * math.log2(math.e)
DEAD = -1e30


class Place:
    def __init__(self):
        self.s = lax.axis_index("seq")
        self.h = lax.axis_index("head")
        self.z = self.s // 8
        self.xl = lax.rem(self.s // 4, 2)
        self.y = lax.rem(self.s, 4)
        self.xh = self.h // 2
        self.c = lax.rem(self.h, 2)
        self.x = self.xh * 2 + self.xl

    def peer(self, dim, d):
        x, y, z = self.x, self.y, self.z
        if dim == "x":
            x = lax.rem(x + d, 4)
        elif dim == "y":
            y = lax.rem(y + d, 4)
        else:
            z = lax.rem(z + d, 4)
        return (z * 8 + lax.rem(x, 2) * 4 + y, (x // 2) * 2 + self.c)

    def sibling(self):
        return (self.s, self.xh * 2 + 1 - self.c)


def duty(s):
    z, xl, y = s // 8, lax.rem(s // 4, 2), lax.rem(s, 4)
    r = lax.rem(y + z, 4)
    return z * 3 + r, xl, r < 3


def remote(src, dst, send, recv, device):
    return pltpu.make_async_remote_copy(
        src_ref=src, dst_ref=dst, send_sem=send, recv_sem=recv, device_id=device, device_id_type=MESH
    )


def greet(barrier, device):
    pl.semaphore_signal(barrier, inc=1, device_id=device, device_id_type=MESH)


def project_kernel(
    x_ref, w_ref, len_ref, kc_ref, vc_ref, qkv_ref,
    other, theirs, slab, weight, outbox,
    pair_sem, one_send, one_recv, two_send, two_recv, three_send, three_recv, own_sem, box_send, box_recv,
):
    me = Place()
    barrier = pltpu.get_barrier_semaphore()

    def greet_seq(i, carry):
        greet(barrier, (lax.rem(me.s + i, 32), me.h))
        return carry

    lax.fori_loop(1, 32, greet_seq, 0)
    greet(barrier, me.sibling())
    for xl in range(2):
        greet(barrier, (me.z * 8 + xl * 4 + me.y, (1 - me.xh) * 2 + me.c))

    for k in range(2):
        for t in range(3):
            at = pl.multiple_of(t * 1024 + (2 * k + 1 - me.c) * 256, 256)
            other[:, k * 768 + t * 256 : k * 768 + (t + 1) * 256] = w_ref[:, pl.ds(at, 256)]
    pl.semaphore_wait(barrier, 34)
    swap = remote(other, theirs, pair_sem.at[0], pair_sem.at[1], me.sibling())
    swap.start()
    swap.wait()
    first = me.c == 0
    for k in range(2):
        for t in range(3):
            at = pl.multiple_of(t * 1024 + (2 * k + me.c) * 256, 256)
            mine = w_ref[:, pl.ds(at, 256)]
            sent = theirs[:, k * 768 + t * 256 : k * 768 + (t + 1) * 256]
            rows = jnp.concatenate([jnp.where(first, mine, sent), jnp.where(first, sent, mine)], axis=0)
            slab[k, :, t * 256 : (t + 1) * 256] = rows.astype(BF)
    weight[me.z, me.xl, me.y, me.xh] = slab[me.xh]

    one = []
    for d in range(1, 4):
        target = me.peer("x", d)
        copy = remote(
            slab.at[target[1] // 2],
            weight.at[me.z, me.xl, me.y, me.xh],
            one_send.at[d - 1],
            one_recv.at[d - 1],
            target,
        )
        copy.start()
        one.append(copy)
    for copy in one:
        copy.wait_recv()

    left, right = pl.ds(0, 384), pl.ds(384, 384)
    all2, all4, all16 = pl.ds(0, 2), pl.ds(0, 4), pl.ds(0, 16)
    zs, ys = pl.ds(me.z, 1), pl.ds(me.y, 1)
    two = []
    for d in range(1, 4):
        for k, (dim, cols) in enumerate((("y", left), ("z", right))):
            part = weight.at[zs, all2, ys, all2, all16, cols]
            copy = remote(part, part, two_send.at[k, d - 1], two_recv.at[k, d - 1], me.peer(dim, d))
            copy.start()
            two.append(copy)
    for copy in two:
        copy.wait_recv()
    three = []
    for d in range(1, 4):
        for k, dim in enumerate(("z", "y")):
            if k == 0:
                part = weight.at[zs, all2, all4, all2, all16, left]
            else:
                part = weight.at[all4, all2, ys, all2, all16, right]
            copy = remote(part, part, three_send.at[k, d - 1], three_recv.at[k, d - 1], me.peer(dim, d))
            copy.start()
            three.append(copy)
    for copy in three:
        copy.wait_recv()

    for t in range(3):
        w = weight[:, :, :, :, :, t * 256 : (t + 1) * 256].reshape(1024, 256)
        for g in range(2):
            rows = x_ref[g * 6 : (g + 1) * 6].reshape(384, 1024)
            got = jnp.dot(rows, w, preferred_element_type=F32)
            for q in range(6):
                p = g * 6 + q
                piece = got[q * 64 : (q + 1) * 64]
                if t > 0:
                    at = me.s * 64 + lax.broadcasted_iota(jnp.int32, (64, 256), 0)
                    piece = jnp.where(at < len_ref[p], piece, 0.0)
                piece = piece.astype(BF)
                if t == 1:
                    kc_ref[p] = piece
                if t == 2:
                    vc_ref[p] = piece
                outbox[p * 2, t] = piece[:, :128]
                outbox[p * 2 + 1, t] = piece[:, 128:]

    prompt, pair, busy = duty(me.s)

    def post(i, carry):
        to = lax.rem(me.s + i, 32)
        their_prompt, their_pair, their_busy = duty(to)

        @pl.when(their_busy)
        def _():
            remote(
                outbox.at[their_prompt * 2 + their_pair], qkv_ref.at[:, me.s], box_send, box_recv, (to, me.h)
            ).start()

        return carry

    lax.fori_loop(1, 32, post, 0)

    @pl.when(busy)
    def _():
        keep = pltpu.make_async_copy(outbox.at[prompt * 2 + pair], qkv_ref.at[:, me.s], own_sem)
        keep.start()
        keep.wait()
        arrived = qkv_ref.at[:, pl.ds(0, 31)]
        pltpu.make_async_copy(arrived, arrived, box_recv).wait()
        gone = outbox.at[pl.ds(0, 23)]
        pltpu.make_async_copy(gone, gone, box_send).wait()

    @pl.when(jnp.logical_not(busy))
    def _():
        gone = outbox.at[pl.ds(0, 24)]
        pltpu.make_async_copy(gone, gone, box_send).wait()

    for copy in one + two + three:
        copy.wait_send()


def project(x, w_qkv, lengths):
    vmem, hbm = pl.BlockSpec(memory_space=pltpu.VMEM), pl.BlockSpec(memory_space=pl.ANY)
    dma = pltpu.SemaphoreType.DMA
    return pl.pallas_call(
        project_kernel,
        out_shape=(
            jax.ShapeDtypeStruct((12, 64, 256), BF),
            jax.ShapeDtypeStruct((12, 64, 256), BF),
            jax.ShapeDtypeStruct((3, 32, 64, 128), BF),
        ),
        in_specs=[vmem, vmem, pl.BlockSpec(memory_space=pltpu.SMEM)],
        out_specs=(vmem, vmem, hbm),
        scratch_shapes=[
            pltpu.VMEM((8, 1536), F32),
            pltpu.VMEM((8, 1536), F32),
            pltpu.VMEM((2, 16, 768), BF),
            pltpu.VMEM((4, 2, 4, 2, 16, 768), BF),
            pltpu.VMEM((24, 3, 64, 128), BF),
            dma((2,)),
            dma((3,)),
            dma((3,)),
            dma((2, 3)),
            dma((2, 3)),
            dma((2, 3)),
            dma((2, 3)),
            dma,
            dma,
            dma,
        ],
        compiler_params=pltpu.CompilerParams(collective_id=0, has_side_effects=True, vmem_limit_bytes=48 << 20),
    )(x, w_qkv, lengths)


def normalize(rows, gain, shift):
    average = jnp.mean(rows, axis=1, keepdims=True)
    spread = jnp.mean(rows * rows, axis=1, keepdims=True) - average * average
    return (rows - average) * lax.rsqrt(spread + EPSILON) * gain + shift


def layer_kernel(
    qkv_ref, x_ref, len_ref, out_f32, in_f32, down_f32, gain_ref, bias_ref, hidden_ref,
    in_half, out_half, w_in, w_out, w_down, q_aug, k_aug, v_aug, attended, joined, hidden, result,
    swap_send, swap_recv, ring_send, ring_recv, share_send, share_recv,
    mix_send, mix_recv, mix_own, last_send, last_recv,
):
    me = Place()
    prompt, pair, busy = duty(me.s)
    barrier = pltpu.get_barrier_semaphore()
    rank = me.s * 4 + me.h

    def greet_all(i, carry):
        to = lax.rem(rank + i, 128)
        greet(barrier, (to // 4, lax.rem(to, 4)))
        return carry

    lax.fori_loop(1, 128, greet_all, 0)
    pl.semaphore_wait(barrier, 127)

    sibling = me.sibling()
    there = 1 - me.c
    swaps = [
        remote(
            out_f32.at[:, pl.ds(pl.multiple_of(there * 512, 512), 512)],
            out_half, swap_send.at[0], swap_recv.at[0], sibling,
        ),
        remote(
            in_f32.at[:, pl.ds(pl.multiple_of(there * 2048, 2048), 2048)],
            in_half, swap_send.at[1], swap_recv.at[1], sibling,
        ),
    ]
    for copy in swaps:
        copy.start()
    w_down[me.z, me.xl, me.y, me.xh, me.c] = down_f32[...].astype(BF)
    for copy in swaps:
        copy.wait_recv()
    first = me.c == 0
    for source, half, width, target in ((out_f32, out_half, 512, w_out), (in_f32, in_half, 2048, w_in)):
        mine = source[:, pl.ds(pl.multiple_of(me.c * width, width), width)]
        sent = half[...]
        rows = jnp.concatenate([jnp.where(first, mine, sent), jnp.where(first, sent, mine)], axis=0)
        target[me.c, me.z, me.xl, me.y, me.xh] = rows.astype(BF)

    one_c = pl.ds(me.c, 1)

    def region(piece, zs, xls, ys, xhs):
        rows16, rows32 = pl.ds(0, 16), pl.ds(0, 32)
        if piece == 0:
            return w_in.at[one_c, zs, xls, ys, xhs, rows16, pl.ds(0, 1536)]
        if piece == 1:
            return w_out.at[one_c, zs, xls, ys, xhs, rows16, pl.ds(0, 512)]
        if piece == 2:
            return w_in.at[one_c, zs, xls, ys, xhs, rows16, pl.ds(1536, 512)]
        if piece == 3:
            return w_down.at[zs, xls, ys, xhs, one_c, rows32, pl.ds(768, 256)]
        return w_down.at[zs, xls, ys, xhs, one_c, rows32, pl.ds(0, 768)]

    order = {0: "xyz", 1: "yzx", 2: "yzx", 3: "yzx", 4: "zxy"}
    pieces = (1, 0, 2, 3, 4)

    def area(piece, done, at=None):
        x, y, z = me.x, me.y, me.z
        if at is not None:
            dim, d = at
            x = lax.rem(x + d, 4) if dim == "x" else x
            y = lax.rem(y + d, 4) if dim == "y" else y
            z = lax.rem(z + d, 4) if dim == "z" else z
        zs = pl.ds(0, 4) if "z" in done else pl.ds(z, 1)
        ys = pl.ds(0, 4) if "y" in done else pl.ds(y, 1)
        xls = pl.ds(0, 2) if "x" in done else pl.ds(lax.rem(x, 2), 1)
        xhs = pl.ds(0, 2) if "x" in done else pl.ds(x // 2, 1)
        return region(piece, zs, xls, ys, xhs)

    pending = []

    def send_phase(phase):
        started = []
        for piece in pieces:
            dims = order[piece]
            part = area(piece, dims[:phase])
            for d in (1, 3, 2):
                copy = remote(
                    part, part, ring_send.at[piece, phase, d - 1], ring_recv.at[piece, phase, d - 1],
                    me.peer(dims[phase], d),
                )
                copy.start()
                started.append((piece, d, copy))
                pending.append(copy)
        return started

    shares = []

    def share(piece, slot, part):
        copy = remote(part, part, share_send.at[piece, slot], share_recv.at[piece, slot], sibling)
        copy.start()
        shares.append(copy)
        pending.append(copy)

    lane = lax.broadcasted_iota(jnp.int32, (2048, 128), 1)

    @pl.when(busy)
    def _():
        place = lax.broadcasted_iota(jnp.int32, (2048, 128), 0)
        bias = jnp.where(place < len_ref[prompt], 0.0, DEAD)
        q = qkv_ref[0].reshape(2048, 128).astype(F32)
        k = qkv_ref[1].reshape(2048, 128).astype(F32)
        v = qkv_ref[2].reshape(2048, 128).astype(F32)
        for n in range(2):
            own = (lane // 64) == n
            mark = lane == (1 - n) * 64
            q_aug[n] = jnp.where(own, q, jnp.where(mark, 1.0, 0.0)).astype(BF)
            k_aug[n] = jnp.where(mark, bias, k).astype(BF)
            v_aug[n] = jnp.where(own, v, 1.0).astype(BF)

    low = lax.broadcasted_iota(jnp.int32, (256, 128), 1) < 64

    def attend(start, stop):
        @pl.when(busy)
        def _():
            def block(i, carry):
                rows = pl.ds(pl.multiple_of(i * 256, 256), 256)
                mixed = []
                for n in range(2):
                    scores = lax.dot_general(
                        q_aug[n, rows, :], k_aug[n], (((1,), (1,)), ((), ())), preferred_element_type=F32
                    )
                    top = jnp.max(scores, axis=1, keepdims=True)
                    terms = jnp.exp2((scores - top) * SCORE_FACTOR).astype(BF)
                    got = jnp.dot(terms, v_aug[n], preferred_element_type=F32)
                    mixed.append(got / pltpu.roll(got, 64, 1))
                both = jnp.where(low, mixed[0], mixed[1]).astype(BF)
                attended[pl.ds(i * 4, 4)] = both.reshape(4, 64, 128)
                return carry

            lax.fori_loop(start, stop, block, 0)

    started = send_phase(0)
    attend(0, 1)
    for _, _, copy in started:
        copy.wait_recv()
    started = send_phase(1)
    attend(1, 3)
    for _, _, copy in started:
        copy.wait_recv()
    started = send_phase(2)
    for piece in pieces:
        share(piece, 0, area(piece, order[piece][:2]))
    attend(3, 8)

    columns = pl.ds(pl.multiple_of((me.h * 2 + pair) * 128, 128), 128)
    slot = lax.rem(prompt, 3)
    lands_here = me.h == me.z

    @pl.when(busy)
    def _():
        def post(i, carry):
            to = lax.rem(me.s + i, 32)
            remote(
                attended.at[to], joined.at[slot, :, columns], mix_send, mix_recv, (to, me.z)
            ).start()
            return carry

        lax.fori_loop(1, 32, post, 0)

        @pl.when(lands_here)
        def _():
            keep = pltpu.make_async_copy(attended.at[me.s], joined.at[slot, :, columns], mix_own)
            keep.start()
            keep.wait()

        @pl.when(jnp.logical_not(lands_here))
        def _():
            remote(
                attended.at[me.s], joined.at[slot, :, columns], mix_send, mix_recv, (me.s, me.z)
            ).start()

    for piece, d, copy in started:
        copy.wait_recv()
        dims = order[piece]
        share(piece, d, area(piece, dims[:2], (dims[2], 4 - d)))

    mine_too = jnp.logical_and(busy, lands_here)

    @pl.when(mine_too)
    def _():
        part = attended.at[pl.ds(0, 23)]
        pltpu.make_async_copy(part, part, mix_recv).wait()

    @pl.when(jnp.logical_not(mine_too))
    def _():
        part = attended.at[pl.ds(0, 24)]
        pltpu.make_async_copy(part, part, mix_recv).wait()

    for copy in shares:
        copy.wait_recv()

    x_rows = x_ref[pl.ds(me.h * 3, 3)].reshape(192, 1024).astype(F32)
    mixed = joined[...].reshape(192, 1024)
    sums = jnp.concatenate(
        [jnp.dot(mixed, w_out[n].reshape(1024, 512), preferred_element_type=F32) for n in range(2)], axis=1
    )
    normed = normalize(sums + x_rows, gain_ref[0:1], bias_ref[0:1]).astype(BF)
    for n in range(2):
        for k in range(4):
            w = w_in[n, :, :, :, :, :, k * 512 : (k + 1) * 512].reshape(1024, 512)
            units = jnp.dot(normed, w, preferred_element_type=F32)
            units = 0.5 * units * (1.0 + lax.erf(units * (2.0**-0.5)))
            hidden[n * 4 + k] = units.astype(BF)
    total = normed.astype(F32)
    for k in range(8):
        w = w_down[k // 2, k % 2].reshape(512, 1024)
        total = total + jnp.dot(hidden[k], w, preferred_element_type=F32)
    final = normalize(total, gain_ref[1:2], bias_ref[1:2]).astype(BF)
    for n in range(4):
        result[n] = final[:, n * 256 : (n + 1) * 256].reshape(3, 64, 256)
    rows = pl.ds(me.h * 3, 3)
    hidden_ref[rows] = result[me.h]
    last = []
    for d in range(1, 4):
        to = lax.rem(me.h + d, 4)
        copy = remote(result.at[to], hidden_ref.at[rows], last_send.at[d - 1], last_recv.at[d - 1], (me.s, to))
        copy.start()
        last.append(copy)

    @pl.when(jnp.logical_and(busy, lands_here))
    def _():
        part = attended.at[pl.ds(0, 31)]
        pltpu.make_async_copy(part, part, mix_send).wait()

    @pl.when(jnp.logical_and(busy, jnp.logical_not(lands_here)))
    def _():
        pltpu.make_async_copy(attended, attended, mix_send).wait()

    for copy in swaps + pending:
        copy.wait_send()
    for copy in last:
        copy.wait()


def layer(qkv, x, lengths, w_attn_out, w_in, w_down, ln_gain, ln_bias):
    vmem = pl.BlockSpec(memory_space=pltpu.VMEM)
    dma = pltpu.SemaphoreType.DMA
    return pl.pallas_call(
        layer_kernel,
        out_shape=jax.ShapeDtypeStruct((12, 64, 256), BF),
        in_specs=[vmem, vmem, pl.BlockSpec(memory_space=pltpu.SMEM)] + [vmem] * 5,
        out_specs=vmem,
        scratch_shapes=[
            pltpu.VMEM((8, 2048), F32),
            pltpu.VMEM((8, 512), F32),
            pltpu.VMEM((2, 4, 2, 4, 2, 16, 2048), BF),
            pltpu.VMEM((2, 4, 2, 4, 2, 16, 512), BF),
            pltpu.VMEM((4, 2, 4, 2, 2, 32, 1024), BF),
            pltpu.VMEM((2, 2048, 128), BF),
            pltpu.VMEM((2, 2048, 128), BF),
            pltpu.VMEM((2, 2048, 128), BF),
            pltpu.VMEM((32, 64, 128), BF),
            pltpu.VMEM((3, 64, 1024), BF),
            pltpu.VMEM((8, 192, 512), BF),
            pltpu.VMEM((4, 3, 64, 256), BF),
            dma((2,)),
            dma((2,)),
            dma((5, 3, 3)),
            dma((5, 3, 3)),
            dma((5, 4)),
            dma((5, 4)),
            dma,
            dma,
            dma,
            dma((3,)),
            dma((3,)),
        ],
        compiler_params=pltpu.CompilerParams(collective_id=1, has_side_effects=True, vmem_limit_bytes=58 << 20),
    )(qkv, x, lengths, w_attn_out, w_in, w_down, ln_gain, ln_bias)


def per_device(hidden_in, lengths, w_qkv, w_attn_out, w_in, w_down, ln_gain, ln_bias):
    key_cache, value_cache, qkv = project(hidden_in, w_qkv, lengths)
    hidden_out = layer(qkv, hidden_in, lengths, w_attn_out, w_in, w_down, ln_gain, ln_bias)
    return (hidden_out, key_cache, value_cache)


def solution(mesh):
    rows = P(("seq", "head"), None)
    in_specs = (P(None, "seq", None), P(), rows, rows, rows, rows, P(), P())
    out_specs = (P(None, "seq", "head"),) * 3
    return jax.shard_map(per_device, mesh=mesh, in_specs=in_specs, out_specs=out_specs, check_vma=False)
```

time: 1290 us -> 148 us (0.11)
  waiting for transfers between devices: 905 us -> 0 us
  blocking collectives: 140 us -> 0 us
  Pallas kernels: 0 us -> 139 us
  matrix products: 86.7 us -> 0 us
  local copies, waits for them, and re-layouts: 84.7 us -> 7.37 us
  starting transfers between devices: 43.3 us -> 0 us
  between operations: 14.4 us -> 0.67 us
    all_gather x7 -> x0, waiting for transfers between devices: 842 us -> none  [the longest x1 275 us: per_device(): lax.all_gather(values_here, 'seq', axis=1, tiled=True)]
    pallas_call x0 -> x2, Pallas kernels: none -> 139 us  [the longest x1 90.4 us: layer(): pl.pallas_call(layer_kernel, out_shape=jax.ShapeDtypeStruct((12, 64, 256)...]
    while x2 -> x0, local copies, waits for them, and re-layouts: 71.8 us -> none  [per_device(): attended = lax.map(one_prompt, (queries, keys_all, values_all, key_live))]
    all_gather x1 -> x0, blocking collectives: 71 us -> none  [relayout(): lax.all_gather(out_stripe, 'seq', axis=0, tiled=True)]
    all_to_all x1 -> x0, blocking collectives: 54.6 us -> none  [relayout(): lax.all_to_all(gathered[2], 'head', split_axis=1, concat_axis=0, tiled=True)]
    dot_general x15 -> x0, matrix products: 47.4 us -> none  [the longest x12 29.1 us: one_prompt(): jnp.einsum('hqk,khd->qhd', soft_weights, value_rows, preferred_element_ty...]
    all_to_all x2 -> x0, starting transfers between devices: 43.1 us -> none  [the longest x1 25 us: relayout(): lax.all_to_all(gathered[0], 'head', split_axis=1, concat_axis=0, tiled=True)]
    sub x12 -> x0, matrix products: 39.3 us -> none  [one_prompt(): exp_terms = jnp.exp(scores - row_max)]
  transfers between devices with their start and end apart: 10 -> 0, of which waited for: 9 -> 0; matrix products, arithmetic and copies ran while one was open for 4% -> 0% of each run, Pallas kernels for 0% -> 0%
where the time goes in v1:
time: 148 us; the launch traced here: 147 us
  Pallas kernels  139 us (94%)
  local copies, waits for them, and re-layouts  7.37 us (5%)
    pallas_call x1, Pallas kernels, layer(): pl.pallas_call(layer_kernel, out_shape=jax.ShapeDtypeStruct((12, 64, 256)...  90.4 us
    pallas_call x1, Pallas kernels, project(): pl.pallas_call(project_kernel, out_shape=(jax.ShapeDtypeStruct((12, 64, 2...  48.9 us
    unnamed x11, local copies, waits for them, and re-layouts  7.37 us

profile of v1, /device:TPU:1, one launch (start us, length us, event | category | flops | bytes accessed | tf_op | source)
XLA Modules:
  0.0 147.3 jit_solution(3310945377187472958)
XLA Ops:
  0.6 0.0 copy-start
  0.6 1.4 copy-done
  2.0 0.0 copy-start.2
  2.0 0.9 copy-done.2
  2.9 0.0 copy-start.3
  2.9 0.7 copy-done.3
  3.6 48.9 %shard_map.103 = (bf16[12,64,256]{2,1,0:T(8,128)(2,1)S(1)}, bf16[12,64,256]{2,1,0:T(8,128)(2,1)S(1)}, bf16[3,32,64,128]{3,2,1,0:T(8,128)(2,1)S(1)}) custom-call(bf16[12,64,1024]{2,1,0:T(8,128)(2,1)S(1)} %copy-done, f32[8,3072]{1,0:T(8,128)S(1)} %copy-done.2, s32[12]{0:T(128)S(1)} %copy-done.3), custom_call_target="tpu_custom_call" | custom-call | tf_op jit(solution)/shard_map/pallas_call | solution.py:192
  52.5 0.0 copy-start.1
  52.5 1.2 copy-done.1
  53.7 90.4 %shard_map.104 = bf16[12,64,256]{2,1,0:T(8,128)(2,1)} custom-call(bf16[3,32,64,128]{3,2,1,0:T(8,128)(2,1)} %copy-done.1, bf16[12,64,1024]{2,1,0:T(8,128)(2,1)} %x_ref.3, s32[12]{0:T(128)} %len_ref.3, f32[8,1024]{1,0:T(8,128)} %out_f32.1, f32[8,4096]{1,0:T(8,128)} %in_f32.1, f32[32,1024]{1,0:T(8,128)} %down_f32.1, f32[2,1024]{1,0:T(2,128)} %gain_ref.1, ...), custom_call_target="tpu_custom_call" | custom-call | tf_op jit(solution)/shard_map/pallas_call | solution.py:470
  144.1 1.8 %copy.14 = bf16[12,64,256]{2,1,0:T(8,128)(2,1)} copy(bf16[12,64,256]{2,1,0:T(8,128)(2,1)} %shard_map.104) | data formatting | bytes 786432
  145.8 0.7 copy.15
  146.6 0.7 copy.16
Async XLA Ops:
  0.6 1.4 copy-start
  2.0 0.9 copy-start.2
  2.9 0.7 copy-start.3
  52.5 1.2 copy-start.1

commit v2 on v1

v2 whole, which is shorter than its diff:
```python
import math

import jax
import jax.numpy as jnp
from jax import lax
from jax.experimental import pallas as pl
from jax.experimental.pallas import tpu as pltpu
from jax.sharding import PartitionSpec as P

MESH = pl.DeviceIdType.MESH
BF = jnp.bfloat16
F32 = jnp.float32
EPSILON = 1e-05
SCORE_FACTOR = 64 ** (-0.5) * math.log2(math.e)
DEAD = -1e30
IN_CUT = 1536
DOWN_CUT = 768


class Place:
    def __init__(self):
        self.s = lax.axis_index("seq")
        self.h = lax.axis_index("head")
        self.z = self.s // 8
        self.xl = lax.rem(self.s // 4, 2)
        self.y = lax.rem(self.s, 4)
        self.xh = self.h // 2
        self.c = lax.rem(self.h, 2)
        self.x = self.xh * 2 + self.xl

    def peer(self, dim, d):
        x, y, z = self.x, self.y, self.z
        if dim == "x":
            x = lax.rem(x + d, 4)
        elif dim == "y":
            y = lax.rem(y + d, 4)
        else:
            z = lax.rem(z + d, 4)
        return (z * 8 + lax.rem(x, 2) * 4 + y, (x // 2) * 2 + self.c)

    def sibling(self):
        return (self.s, self.xh * 2 + 1 - self.c)


def duty(s):
    z, xl, y = s // 8, lax.rem(s // 4, 2), lax.rem(s, 4)
    r = lax.rem(y + z, 4)
    return z * 3 + r, xl, r < 3


def remote(src, dst, send, recv, device):
    return pltpu.make_async_remote_copy(
        src_ref=src, dst_ref=dst, send_sem=send, recv_sem=recv, device_id=device, device_id_type=MESH
    )


def greet(barrier, device):
    pl.semaphore_signal(barrier, inc=1, device_id=device, device_id_type=MESH)


def normalize(rows, gain, shift):
    average = jnp.mean(rows, axis=1, keepdims=True)
    spread = jnp.mean(rows * rows, axis=1, keepdims=True) - average * average
    return (rows - average) * lax.rsqrt(spread + EPSILON) * gain + shift


def layer_kernel(
    x_hbm, len_ref, qkv_hbm, out_hbm, in_hbm, down_hbm, gain_ref, bias_ref, hidden_hbm, kc_hbm, vc_hbm,
    x_ref, qkv_f32, out_f32, in_f32, down_f32, other, qkv_half, in_half, out_half,
    slab, w_qkv, w_in, w_out, w_down, outbox, inbox, q_aug, k_aug, v_aug, attended, joined, hidden, result,
    caches, load_sem, swap_send, swap_recv, one_send, one_recv, two_send, two_recv, three_send, three_recv,
    box_own, box_send, box_recv, cache_sem, ring_send, ring_recv, last_ring_send, last_ring_recv,
    share_send, share_recv, mix_send, mix_recv, mix_own, back_send, back_recv, back_own,
):
    me = Place()
    prompt, pair, busy = duty(me.s)
    sibling = me.sibling()
    loads = [
        pltpu.make_async_copy(source, target, load_sem.at[n])
        for n, (source, target) in enumerate(
            (
                (qkv_hbm, qkv_f32), (out_hbm, out_f32), (in_hbm, in_f32), (down_hbm, down_f32), (x_hbm, x_ref),
            )
        )
    ]
    for copy in loads:
        copy.start()
    barrier = pltpu.get_barrier_semaphore()

    def greet_seq(i, carry):
        greet(barrier, (lax.rem(me.s + i, 32), me.h))
        return carry

    greet(barrier, sibling)
    for xl in range(2):
        greet(barrier, (me.z * 8 + xl * 4 + me.y, (1 - me.xh) * 2 + me.c))
    lax.fori_loop(1, 32, greet_seq, 0)

    loads[0].wait()
    for k in range(2):
        for t in range(3):
            at = pl.multiple_of(t * 1024 + (2 * k + 1 - me.c) * 256, 256)
            other[:, k * 768 + t * 256 : k * 768 + (t + 1) * 256] = qkv_f32[:, pl.ds(at, 256)]
    loads[1].wait()
    loads[2].wait()
    there = 1 - me.c
    swaps = [
        remote(other, qkv_half, swap_send.at[0], swap_recv.at[0], sibling),
        remote(
            out_f32.at[:, pl.ds(pl.multiple_of(there * 512, 512), 512)],
            out_half, swap_send.at[1], swap_recv.at[1], sibling,
        ),
        remote(
            in_f32.at[:, pl.ds(pl.multiple_of(there * 2048, 2048), 2048)],
            in_half, swap_send.at[2], swap_recv.at[2], sibling,
        ),
    ]
    pl.semaphore_wait(barrier, 34)
    for copy in swaps:
        copy.start()
    loads[3].wait()
    w_down[me.z, me.xl, me.y, me.xh, me.c] = down_f32[...].astype(BF)
    first = me.c == 0

    def stack(mine, sent):
        rows = jnp.concatenate([jnp.where(first, mine, sent), jnp.where(first, sent, mine)], axis=0)
        return rows.astype(BF)

    swaps[0].wait_recv()
    for k in range(2):
        for t in range(3):
            at = pl.multiple_of(t * 1024 + (2 * k + me.c) * 256, 256)
            cols = slice(k * 768 + t * 256, k * 768 + (t + 1) * 256)
            slab[k, :, t * 256 : (t + 1) * 256] = stack(qkv_f32[:, pl.ds(at, 256)], qkv_half[:, cols])
    w_qkv[me.z, me.xl, me.y, me.xh] = slab[me.xh]
    pending = []
    one = []
    for d in (1, 3, 2):
        target = me.peer("x", d)
        copy = remote(
            slab.at[target[1] // 2], w_qkv.at[me.z, me.xl, me.y, me.xh], one_send.at[d - 1], one_recv.at[d - 1], target
        )
        copy.start()
        one.append(copy)
    pending += one

    for n, (source, half, width, target) in enumerate(
        ((out_f32, out_half, 512, w_out), (in_f32, in_half, 2048, w_in))
    ):
        swaps[n + 1].wait_recv()
        mine = source[:, pl.ds(pl.multiple_of(me.c * width, width), width)]
        target[me.c, me.z, me.xl, me.y, me.xh] = stack(mine, half[...])

    one_c = pl.ds(me.c, 1)

    def region(piece, zs, xls, ys, xhs):
        rows16, rows32 = pl.ds(0, 16), pl.ds(0, 32)
        if piece == 0:
            return w_in.at[one_c, zs, xls, ys, xhs, rows16, pl.ds(0, IN_CUT)]
        if piece == 1:
            return w_out.at[one_c, zs, xls, ys, xhs, rows16, pl.ds(0, 512)]
        if piece == 2:
            return w_in.at[one_c, zs, xls, ys, xhs, rows16, pl.ds(IN_CUT, 2048 - IN_CUT)]
        if piece == 3:
            return w_down.at[zs, xls, ys, xhs, one_c, rows32, pl.ds(DOWN_CUT, 1024 - DOWN_CUT)]
        return w_down.at[zs, xls, ys, xhs, one_c, rows32, pl.ds(0, DOWN_CUT)]

    order = {0: "xyz", 1: "yzx", 2: "yzx", 3: "yzx", 4: "zxy"}
    pieces = (1, 0, 2, 4, 3)

    def area(piece, done, at=None, half=None):
        x, y, z = me.x, me.y, me.z
        if at is not None:
            dim, d = at
            x = lax.rem(x + d, 4) if dim == "x" else x
            y = lax.rem(y + d, 4) if dim == "y" else y
            z = lax.rem(z + d, 4) if dim == "z" else z
        zs = pl.ds(0, 4) if "z" in done else pl.ds(z, 1)
        ys = pl.ds(0, 4) if "y" in done else pl.ds(y, 1)
        xls = pl.ds(0, 2) if "x" in done else pl.ds(lax.rem(x, 2), 1)
        xhs = pl.ds(0, 2) if "x" in done else pl.ds(x // 2, 1)
        if half is not None:
            if "z" in done:
                zs = pl.ds(half * 2, 2)
            else:
                ys = pl.ds(half * 2, 2)
        return region(piece, zs, xls, ys, xhs)

    def send_phase(phase):
        started = []
        for piece in pieces:
            dims = order[piece]
            part = area(piece, dims[:phase])
            for d in (1, 3, 2):
                copy = remote(
                    part, part, ring_send.at[piece, phase, d - 1], ring_recv.at[piece, phase, d - 1],
                    me.peer(dims[phase], d),
                )
                copy.start()
                started.append(copy)
                pending.append(copy)
        return started

    shares = []

    def share(piece, slot, part):
        copy = remote(part, part, share_send.at[piece, slot], share_recv.at[piece, slot], sibling)
        copy.start()
        shares.append(copy)
        pending.append(copy)

    def pass_on(piece, way, step):
        dims = order[piece]
        dim = dims[2]
        half = (step + way) % 2 if step < 2 else way
        back = 3 if way == 0 else 1
        at = None if step < 2 else (dim, back)
        part = area(piece, dims[:2], at, half)
        copy = remote(
            part, part, last_ring_send.at[piece, way, step], last_ring_recv.at[piece, way, step],
            me.peer(dim, 1 if way == 0 else 3),
        )
        copy.start()
        pending.append(copy)
        return copy

    def came(piece, way, step):
        dims = order[piece]
        half = (step + way) % 2 if step < 2 else way
        back = 3 if way == 0 else 1
        return area(piece, dims[:2], (dims[2], back if step < 2 else 2), half)

    rings = {}

    def ring_start(step):
        for piece in pieces:
            for way in range(2):
                rings[piece, way, step] = pass_on(piece, way, step)

    def ring_take(step, forward):
        for piece in pieces:
            for way in range(2):
                rings[piece, way, step].wait_recv()
                if forward:
                    rings[piece, way, 2] = pass_on(piece, way, 2)
                share(piece, 1 + way * 3 + step, came(piece, way, step))

    bulk_one = send_phase(0)
    for copy in one:
        copy.wait_recv()
    left, right = pl.ds(0, 384), pl.ds(384, 384)
    all2, all4, all16 = pl.ds(0, 2), pl.ds(0, 4), pl.ds(0, 16)
    zs, ys = pl.ds(me.z, 1), pl.ds(me.y, 1)
    two = []
    for d in (1, 3, 2):
        for k, (dim, cols) in enumerate((("y", left), ("z", right))):
            part = w_qkv.at[zs, all2, ys, all2, all16, cols]
            copy = remote(part, part, two_send.at[k, d - 1], two_recv.at[k, d - 1], me.peer(dim, d))
            copy.start()
            two.append(copy)
    pending += two
    for copy in bulk_one:
        copy.wait_recv()
    bulk_two = send_phase(1)
    for copy in two:
        copy.wait_recv()
    three = []
    for d in (1, 3, 2):
        for k, dim in enumerate(("z", "y")):
            if k == 0:
                part = w_qkv.at[zs, all2, all4, all2, all16, left]
            else:
                part = w_qkv.at[all4, all2, ys, all2, all16, right]
            copy = remote(part, part, three_send.at[k, d - 1], three_recv.at[k, d - 1], me.peer(dim, d))
            copy.start()
            three.append(copy)
    pending += three
    loads[4].wait()
    for copy in three:
        copy.wait_recv()

    for t in range(3):
        w = w_qkv[:, :, :, :, :, t * 256 : (t + 1) * 256].reshape(1024, 256)
        for g in range(2):
            rows = x_ref[g * 6 : (g + 1) * 6].reshape(384, 1024)
            got = jnp.dot(rows, w, preferred_element_type=F32)
            for q in range(6):
                p = g * 6 + q
                piece = got[q * 64 : (q + 1) * 64]
                if t > 0:
                    at = me.s * 64 + lax.broadcasted_iota(jnp.int32, (64, 256), 0)
                    piece = jnp.where(at < len_ref[p], piece, 0.0)
                piece = piece.astype(BF)
                if t > 0:
                    caches[t - 1, p] = piece
                outbox[p * 2, t] = piece[:, :128]
                outbox[p * 2 + 1, t] = piece[:, 128:]

    def post(i, carry):
        to = lax.rem(me.s + i, 32)
        their_prompt, their_pair, their_busy = duty(to)

        @pl.when(their_busy)
        def _():
            remote(
                outbox.at[their_prompt * 2 + their_pair], inbox.at[:, me.s], box_send, box_recv, (to, me.h)
            ).start()

        return carry

    lax.fori_loop(1, 32, post, 0)
    keeps = [
        pltpu.make_async_copy(caches.at[0], kc_hbm, cache_sem.at[0]),
        pltpu.make_async_copy(caches.at[1], vc_hbm, cache_sem.at[1]),
    ]
    for copy in keeps:
        copy.start()

    for copy in bulk_two:
        copy.wait_recv()
    ring_start(0)
    ring_start(1)
    for piece in pieces:
        share(piece, 0, area(piece, order[piece][:2]))

    @pl.when(busy)
    def _():
        keep = pltpu.make_async_copy(outbox.at[prompt * 2 + pair], inbox.at[:, me.s], box_own)
        keep.start()
        keep.wait()
        arrived = inbox.at[:, pl.ds(0, 31)]
        pltpu.make_async_copy(arrived, arrived, box_recv).wait()
        lane = lax.broadcasted_iota(jnp.int32, (2048, 128), 1)
        place = lax.broadcasted_iota(jnp.int32, (2048, 128), 0)
        bias = jnp.where(place < len_ref[prompt], 0.0, DEAD)
        q = inbox[0].reshape(2048, 128).astype(F32)
        k = inbox[1].reshape(2048, 128).astype(F32)
        v = inbox[2].reshape(2048, 128).astype(F32)
        for n in range(2):
            own = (lane // 64) == n
            mark = lane == (1 - n) * 64
            q_aug[n] = jnp.where(own, q, jnp.where(mark, 1.0, 0.0)).astype(BF)
            k_aug[n] = jnp.where(mark, bias, k).astype(BF)
            v_aug[n] = jnp.where(own, v, 1.0).astype(BF)

    low = lax.broadcasted_iota(jnp.int32, (256, 128), 1) < 64
    columns = pl.ds(pl.multiple_of((me.h * 2 + pair) * 128, 128), 128)
    slot = lax.rem(prompt, 3)
    lands_here = me.h == me.z

    def attend(start, stop):
        @pl.when(busy)
        def _():
            def block(i, carry):
                rows = pl.ds(pl.multiple_of(i * 256, 256), 256)
                mixed = []
                for n in range(2):
                    scores = lax.dot_general(
                        q_aug[n, rows, :], k_aug[n], (((1,), (1,)), ((), ())), preferred_element_type=F32
                    )
                    top = jnp.max(scores, axis=1, keepdims=True)
                    terms = jnp.exp2((scores - top) * SCORE_FACTOR).astype(BF)
                    got = jnp.dot(terms, v_aug[n], preferred_element_type=F32)
                    mixed.append(got / pltpu.roll(got, 64, 1))
                both = jnp.where(low, mixed[0], mixed[1]).astype(BF)
                attended[pl.ds(i * 4, 4)] = both.reshape(4, 64, 128)
                for k in range(4):
                    to = i * 4 + k
                    stays = jnp.logical_and(lands_here, to == me.s)

                    @pl.when(stays)
                    def _():
                        pltpu.make_async_copy(attended.at[to], joined.at[slot, :, columns], mix_own).start()

                    @pl.when(jnp.logical_not(stays))
                    def _():
                        remote(
                            attended.at[to], joined.at[slot, :, columns], mix_send, mix_recv, (to, me.z)
                        ).start()

                return carry

            lax.fori_loop(start, stop, block, 0)

    attend(0, 3)
    ring_take(0, True)
    attend(3, 8)
    ring_take(1, False)
    ring_take(2, False)
    mine_too = jnp.logical_and(busy, lands_here)

    @pl.when(mine_too)
    def _():
        pltpu.make_async_copy(attended.at[me.s], joined.at[slot, :, columns], mix_own).wait()
        part = attended.at[pl.ds(0, 23)]
        pltpu.make_async_copy(part, part, mix_recv).wait()

    @pl.when(jnp.logical_not(mine_too))
    def _():
        part = attended.at[pl.ds(0, 24)]
        pltpu.make_async_copy(part, part, mix_recv).wait()

    for copy in shares:
        copy.wait_recv()

    x_rows = x_ref[pl.ds(me.h * 3, 3)].reshape(192, 1024).astype(F32)
    mixed = joined[...].reshape(192, 1024)
    sums = jnp.concatenate(
        [jnp.dot(mixed, w_out[n].reshape(1024, 512), preferred_element_type=F32) for n in range(2)], axis=1
    )
    normed = normalize(sums + x_rows, gain_ref[0:1], bias_ref[0:1]).astype(BF)
    for n in range(2):
        for k in range(4):
            w = w_in[n, :, :, :, :, :, k * 512 : (k + 1) * 512].reshape(1024, 512)
            units = jnp.dot(normed, w, preferred_element_type=F32)
            units = 0.5 * units * (1.0 + lax.erf(units * (2.0**-0.5)))
            hidden[n * 4 + k] = units.astype(BF)
    total = normed.astype(F32)
    for k in range(8):
        w = w_down[k // 2, k % 2].reshape(512, 1024)
        total = total + jnp.dot(hidden[k], w, preferred_element_type=F32)
    final = normalize(total, gain_ref[1:2], bias_ref[1:2]).astype(BF)
    for n in range(4):
        result[n] = final[:, n * 256 : (n + 1) * 256].reshape(3, 64, 256)
    rows = pl.ds(me.h * 3, 3)
    own = pltpu.make_async_copy(result.at[me.h], hidden_hbm.at[rows], back_own)
    own.start()
    last = []
    for d in range(1, 4):
        to = lax.rem(me.h + d, 4)
        copy = remote(result.at[to], hidden_hbm.at[rows], back_send.at[d - 1], back_recv.at[d - 1], (me.s, to))
        copy.start()
        last.append(copy)

    @pl.when(busy)
    def _():
        gone = outbox.at[pl.ds(0, 23)]
        pltpu.make_async_copy(gone, gone, box_send).wait()

    @pl.when(jnp.logical_not(busy))
    def _():
        gone = outbox.at[pl.ds(0, 24)]
        pltpu.make_async_copy(gone, gone, box_send).wait()

    @pl.when(mine_too)
    def _():
        part = attended.at[pl.ds(0, 31)]
        pltpu.make_async_copy(part, part, mix_send).wait()

    @pl.when(jnp.logical_and(busy, jnp.logical_not(lands_here)))
    def _():
        pltpu.make_async_copy(attended, attended, mix_send).wait()

    for copy in swaps + pending:
        copy.wait_send()
    for copy in keeps:
        copy.wait()
    own.wait()
    for copy in last:
        copy.wait()


def layer(x, lengths, w_qkv, w_attn_out, w_in, w_down, ln_gain, ln_bias):
    vmem, hbm = pl.BlockSpec(memory_space=pltpu.VMEM), pl.BlockSpec(memory_space=pl.ANY)
    dma = pltpu.SemaphoreType.DMA
    return pl.pallas_call(
        layer_kernel,
        out_shape=(jax.ShapeDtypeStruct((12, 64, 256), BF),) * 3,
        in_specs=[hbm, pl.BlockSpec(memory_space=pltpu.SMEM), hbm, hbm, hbm, hbm, vmem, vmem],
        out_specs=(hbm,) * 3,
        scratch_shapes=[
            pltpu.VMEM((12, 64, 1024), BF),
            pltpu.VMEM((8, 3072), F32),
            pltpu.VMEM((8, 1024), F32),
            pltpu.VMEM((8, 4096), F32),
            pltpu.VMEM((32, 1024), F32),
            pltpu.VMEM((8, 1536), F32),
            pltpu.VMEM((8, 1536), F32),
            pltpu.VMEM((8, 2048), F32),
            pltpu.VMEM((8, 512), F32),
            pltpu.VMEM((2, 16, 768), BF),
            pltpu.VMEM((4, 2, 4, 2, 16, 768), BF),
            pltpu.VMEM((2, 4, 2, 4, 2, 16, 2048), BF),
            pltpu.VMEM((2, 4, 2, 4, 2, 16, 512), BF),
            pltpu.VMEM((4, 2, 4, 2, 2, 32, 1024), BF),
            pltpu.VMEM((24, 3, 64, 128), BF),
            pltpu.VMEM((3, 32, 64, 128), BF),
            pltpu.VMEM((2, 2048, 128), BF),
            pltpu.VMEM((2, 2048, 128), BF),
            pltpu.VMEM((2, 2048, 128), BF),
            pltpu.VMEM((32, 64, 128), BF),
            pltpu.VMEM((3, 64, 1024), BF),
            pltpu.VMEM((8, 192, 512), BF),
            pltpu.VMEM((4, 3, 64, 256), BF),
            pltpu.VMEM((2, 12, 64, 256), BF),
            dma((5,)),
            dma((3,)),
            dma((3,)),
            dma((3,)),
            dma((3,)),
            dma((2, 3)),
            dma((2, 3)),
            dma((2, 3)),
            dma((2, 3)),
            dma,
            dma,
            dma,
            dma((2,)),
            dma((5, 2, 3)),
            dma((5, 2, 3)),
            dma((5, 2, 3)),
            dma((5, 2, 3)),
            dma((5, 7)),
            dma((5, 7)),
            dma,
            dma,
            dma,
            dma((3,)),
            dma((3,)),
            dma,
        ],
        compiler_params=pltpu.CompilerParams(collective_id=0, has_side_effects=True, vmem_limit_bytes=58 << 20),
    )(x, lengths, w_qkv, w_attn_out, w_in, w_down, ln_gain, ln_bias)


def per_device(hidden_in, lengths, w_qkv, w_attn_out, w_in, w_down, ln_gain, ln_bias):
    return layer(hidden_in, lengths, w_qkv, w_attn_out, w_in, w_down, ln_gain, ln_bias)


def solution(mesh):
    rows = P(("seq", "head"), None)
    in_specs = (P(None, "seq", None), P(), rows, rows, rows, rows, P(), P())
    out_specs = (P(None, "seq", "head"),) * 3
    return jax.shard_map(per_device, mesh=mesh, in_specs=in_specs, out_specs=out_specs, check_vma=False)
```

time: 148 us -> 114 us (0.77)
  Pallas kernels: 139 us -> 108 us
  local copies, waits for them, and re-layouts: 7.37 us -> 4.33 us
    pallas_call x2 -> x1, Pallas kernels: 139 us -> 108 us  [layer(): pl.pallas_call(layer_kernel, out_shape=(jax.ShapeDtypeStruct((12, 64, 256...]
    unnamed x11 -> x5, local copies, waits for them, and re-layouts: 7.37 us -> 4.33 us
where the time goes in v2:
time: 114 us; the launch traced here: 113 us
  Pallas kernels  108 us (95%)
  local copies, waits for them, and re-layouts  4.33 us (4%)
    pallas_call x1, Pallas kernels, layer(): pl.pallas_call(layer_kernel, out_shape=(jax.ShapeDtypeStruct((12, 64, 256...  108 us
    unnamed x5, local copies, waits for them, and re-layouts  4.33 us

profile of v2, /device:TPU:1, one launch (start us, length us, event | category | flops | bytes accessed | tf_op | source)
XLA Modules:
  0.0 113.5 jit_solution(13302546855890096339)
XLA Ops:
  0.6 108.5 %shard_map.103 = (bf16[12,64,256]{2,1,0:T(8,128)(2,1)}, bf16[12,64,256]{2,1,0:T(8,128)(2,1)}, bf16[12,64,256]{2,1,0:T(8,128)(2,1)}) custom-call(bf16[12,64,1024]{2,1,0:T(8,128)(2,1)} %x_hbm.1, s32[12]{0:T(128)} %len_ref.1, f32[8,3072]{1,0:T(8,128)} %qkv_hbm.1, f32[8,1024]{1,0:T(8,128)} %out_hbm.1, f32[8,4096]{1,0:T(8,128)} %in_hbm.1, f32[32,1024]{1,0:T(8,128)} %down_hbm.1, ...), custom_call_target="tpu_custom_call" | custom-call | tf_op jit(solution)/shard_map/pallas_call | solution.py:466
  109.1 0.0 copy-start
  109.1 1.8 %copy.14 = bf16[12,64,256]{2,1,0:T(8,128)(2,1)} copy(bf16[12,64,256]{2,1,0:T(8,128)(2,1)} %get-tuple-element.6) | data formatting | bytes 786432
  111.0 1.8 %copy.15 = bf16[12,64,256]{2,1,0:T(8,128)(2,1)} copy(bf16[12,64,256]{2,1,0:T(8,128)(2,1)} %get-tuple-element.7) | data formatting | bytes 786432
  112.7 0.0 copy-done
  112.7 0.7 copy.16
Async XLA Ops:
  109.1 3.6 %copy-start = (bf16[12,64,256]{2,1,0:T(8,128)(2,1)S(1)}, bf16[12,64,256]{2,1,0:T(8,128)(2,1)}, u32[]{:S(2)}) copy-start(bf16[12,64,256]{2,1,0:T(8,128)(2,1)} %get-tuple-element.8) | copy-start | bytes 1179652

commit v3 on v2

--- a/solution.py
+++ b/solution.py
@@ -13,8 +13,8 @@
 EPSILON = 1e-05
 SCORE_FACTOR = 64 ** (-0.5) * math.log2(math.e)
 DEAD = -1e30
-IN_CUT = 1536
-DOWN_CUT = 768
+IN_X, IN_Z = 384, 768
+DOWN_X, DOWN_Z = 512, 256
 
 
 class Place:
@@ -54,6 +54,28 @@
     )
 
 
+class Ring:
+    def __init__(self, me, view, dim, send, recv):
+        self.me, self.view, self.dim, self.send, self.recv = me, view, dim, send, recv
+        self.copies = {}
+
+    def half(self, way, step):
+        return (step + way) % 2 if step < 2 else way
+
+    def go(self, way, step):
+        behind = 3 if way == 0 else 1
+        part = self.view(0 if step < 2 else behind, self.half(way, step))
+        copy = remote(
+            part, part, self.send(way, step), self.recv(way, step), self.me.peer(self.dim, 1 if way == 0 else 3)
+        )
+        copy.start()
+        self.copies[way, step] = copy
+
+    def came(self, way, step):
+        behind = 3 if way == 0 else 1
+        return self.view(behind if step < 2 else 2, self.half(way, step))
+
+
 def greet(barrier, device):
     pl.semaphore_signal(barrier, inc=1, device_id=device, device_id_type=MESH)
 
@@ -69,7 +91,7 @@
     x_ref, qkv_f32, out_f32, in_f32, down_f32, other, qkv_half, in_half, out_half,
     slab, w_qkv, w_in, w_out, w_down, outbox, inbox, q_aug, k_aug, v_aug, attended, joined, hidden, result,
     caches, load_sem, swap_send, swap_recv, one_send, one_recv, two_send, two_recv, three_send, three_recv,
-    box_own, box_send, box_recv, cache_sem, ring_send, ring_recv, last_ring_send, last_ring_recv,
+    box_own, box_send, box_recv, cache_sem, first_send, first_recv, ring_send, ring_recv,
     share_send, share_recv, mix_send, mix_recv, mix_own, back_send, back_recv, back_own,
 ):
     me = Place()
@@ -156,17 +178,19 @@
     def region(piece, zs, xls, ys, xhs):
         rows16, rows32 = pl.ds(0, 16), pl.ds(0, 32)
         if piece == 0:
-            return w_in.at[one_c, zs, xls, ys, xhs, rows16, pl.ds(0, IN_CUT)]
-        if piece == 1:
             return w_out.at[one_c, zs, xls, ys, xhs, rows16, pl.ds(0, 512)]
-        if piece == 2:
-            return w_in.at[one_c, zs, xls, ys, xhs, rows16, pl.ds(IN_CUT, 2048 - IN_CUT)]
-        if piece == 3:
-            return w_down.at[zs, xls, ys, xhs, one_c, rows32, pl.ds(DOWN_CUT, 1024 - DOWN_CUT)]
-        return w_down.at[zs, xls, ys, xhs, one_c, rows32, pl.ds(0, DOWN_CUT)]
-
-    order = {0: "xyz", 1: "yzx", 2: "yzx", 3: "yzx", 4: "zxy"}
-    pieces = (1, 0, 2, 4, 3)
+        start, stop = cuts[piece]
+        if piece < 4:
+            return w_in.at[one_c, zs, xls, ys, xhs, rows16, pl.ds(start, stop - start)]
+        return w_down.at[zs, xls, ys, xhs, one_c, rows32, pl.ds(start, stop - start)]
+
+    cuts = {
+        1: (0, IN_X), 2: (IN_X, IN_X + IN_Z), 3: (IN_X + IN_Z, 2048),
+        4: (0, DOWN_X), 5: (DOWN_X, DOWN_X + DOWN_Z), 6: (DOWN_X + DOWN_Z, 1024),
+    }
+    order = {0: "yzx", 1: "yzx", 2: "xyz", 3: "zxy", 4: "yzx", 5: "xyz", 6: "zxy"}
+    early, late = (0, 1, 2, 3), (4, 5, 6)
+    pieces = early + late
 
     def area(piece, done, at=None, half=None):
         x, y, z = me.x, me.y, me.z
@@ -182,70 +206,68 @@
         if half is not None:
             if "z" in done:
                 zs = pl.ds(half * 2, 2)
+            elif "y" in done:
+                ys = pl.ds(half * 2, 2)
             else:
-                ys = pl.ds(half * 2, 2)
+                xls = pl.ds(half, 1)
         return region(piece, zs, xls, ys, xhs)
 
-    def send_phase(phase):
+    def send_first():
         started = []
         for piece in pieces:
-            dims = order[piece]
-            part = area(piece, dims[:phase])
+            part = area(piece, "")
             for d in (1, 3, 2):
                 copy = remote(
-                    part, part, ring_send.at[piece, phase, d - 1], ring_recv.at[piece, phase, d - 1],
-                    me.peer(dims[phase], d),
+                    part, part, first_send.at[piece, d - 1], first_recv.at[piece, d - 1], me.peer(order[piece][0], d)
                 )
                 copy.start()
                 started.append(copy)
                 pending.append(copy)
         return started
 
-    shares = []
+    shares = {}
 
     def share(piece, slot, part):
         copy = remote(part, part, share_send.at[piece, slot], share_recv.at[piece, slot], sibling)
         copy.start()
-        shares.append(copy)
+        shares[piece, slot] = copy
         pending.append(copy)
 
-    def pass_on(piece, way, step):
-        dims = order[piece]
-        dim = dims[2]
-        half = (step + way) % 2 if step < 2 else way
-        back = 3 if way == 0 else 1
-        at = None if step < 2 else (dim, back)
-        part = area(piece, dims[:2], at, half)
-        copy = remote(
-            part, part, last_ring_send.at[piece, way, step], last_ring_recv.at[piece, way, step],
-            me.peer(dim, 1 if way == 0 else 3),
-        )
-        copy.start()
-        pending.append(copy)
-        return copy
-
-    def came(piece, way, step):
-        dims = order[piece]
-        half = (step + way) % 2 if step < 2 else way
-        back = 3 if way == 0 else 1
-        return area(piece, dims[:2], (dims[2], back if step < 2 else 2), half)
-
     rings = {}
-
-    def ring_start(step):
-        for piece in pieces:
+    for piece in pieces:
+        for phase in (1, 2):
+            dims = order[piece]
+            rings[piece, phase] = Ring(
+                me,
+                lambda d, half, piece=piece, dims=dims, phase=phase: area(piece, dims[:phase], (dims[phase], d), half),
+                dims[phase],
+                lambda way, step, piece=piece, phase=phase: ring_send.at[piece, phase - 1, way, step],
+                lambda way, step, piece=piece, phase=phase: ring_recv.at[piece, phase - 1, way, step],
+            )
+
+    def start(which, step):
+        for ring in which:
             for way in range(2):
-                rings[piece, way, step] = pass_on(piece, way, step)
-
-    def ring_take(step, forward):
-        for piece in pieces:
+                ring.go(way, step)
+
+    def take(which, step):
+        for ring in which:
             for way in range(2):
-                rings[piece, way, step].wait_recv()
-                if forward:
-                    rings[piece, way, 2] = pass_on(piece, way, 2)
-                share(piece, 1 + way * 3 + step, came(piece, way, step))
-
-    bulk_one = send_phase(0)
+                ring.copies[way, step].wait_recv()
+                if step == 0:
+                    ring.go(way, 2)
+
+    def ring_start(group, step):
+        start([rings[piece, 2] for piece in group], step)
+
+    def ring_take(group, step):
+        for piece in group:
+            ring = rings[piece, 2]
+            take([ring], step)
+            for way in range(2):
+                share(piece, 1 + way * 3 + step, ring.came(way, step))
+
+    bulk_one = send_first()
     for copy in one:
         copy.wait_recv()
     left, right = pl.ds(0, 384), pl.ds(384, 384)
@@ -261,23 +283,33 @@
     pending += two
     for copy in bulk_one:
         copy.wait_recv()
-    bulk_two = send_phase(1)
+    middle = [rings[piece, 1] for piece in pieces]
+    start(middle, 0)
+    start(middle, 1)
     for copy in two:
         copy.wait_recv()
-    three = []
-    for d in (1, 3, 2):
-        for k, dim in enumerate(("z", "y")):
-            if k == 0:
-                part = w_qkv.at[zs, all2, all4, all2, all16, left]
-            else:
-                part = w_qkv.at[all4, all2, ys, all2, all16, right]
-            copy = remote(part, part, three_send.at[k, d - 1], three_recv.at[k, d - 1], me.peer(dim, d))
-            copy.start()
-            three.append(copy)
-    pending += three
+
+    def view_left(d, half):
+        return w_qkv.at[pl.ds(lax.rem(me.z + d, 4), 1), all2, pl.ds(half * 2, 2), all2, all16, left]
+
+    def view_right(d, half):
+        return w_qkv.at[pl.ds(half * 2, 2), all2, pl.ds(lax.rem(me.y + d, 4), 1), all2, all16, right]
+
+    three = [
+        Ring(
+            me, view, dim,
+            lambda way, step, k=k: three_send.at[k, way, step],
+            lambda way, step, k=k: three_recv.at[k, way, step],
+        )
+        for k, (view, dim) in enumerate(((view_left, "z"), (view_right, "y")))
+    ]
+    start(three, 0)
+    start(three, 1)
+    take(three, 0)
+    take(middle, 0)
     loads[4].wait()
-    for copy in three:
-        copy.wait_recv()
+    take(three, 1)
+    take(three, 2)
 
     for t in range(3):
         w = w_qkv[:, :, :, :, :, t * 256 : (t + 1) * 256].reshape(1024, 256)
@@ -316,12 +348,16 @@
     for copy in keeps:
         copy.start()
 
-    for copy in bulk_two:
-        copy.wait_recv()
-    ring_start(0)
-    ring_start(1)
+    take(middle, 1)
+    take(middle, 2)
+    ring_start(early, 0)
+    ring_start(early, 1)
     for piece in pieces:
         share(piece, 0, area(piece, order[piece][:2]))
+    ring_take(early, 0)
+    ring_start(late, 0)
+    ring_take(early, 1)
+    ring_start(late, 1)
 
     @pl.when(busy)
     def _():
@@ -382,11 +418,12 @@
 
             lax.fori_loop(start, stop, block, 0)
 
-    attend(0, 3)
-    ring_take(0, True)
-    attend(3, 8)
-    ring_take(1, False)
-    ring_take(2, False)
+    attend(0, 2)
+    ring_take(early, 2)
+    attend(2, 6)
+    ring_take(late, 0)
+    attend(6, 8)
+    ring_take(late, 1)
     mine_too = jnp.logical_and(busy, lands_here)
 
     @pl.when(mine_too)
@@ -400,8 +437,9 @@
         part = attended.at[pl.ds(0, 24)]
         pltpu.make_async_copy(part, part, mix_recv).wait()
 
-    for copy in shares:
-        copy.wait_recv()
+    for key, copy in shares.items():
+        if key[0] in early:
+            copy.wait_recv()
 
     x_rows = x_ref[pl.ds(me.h * 3, 3)].reshape(192, 1024).astype(F32)
     mixed = joined[...].reshape(192, 1024)
@@ -415,6 +453,10 @@
             units = jnp.dot(normed, w, preferred_element_type=F32)
             units = 0.5 * units * (1.0 + lax.erf(units * (2.0**-0.5)))
             hidden[n * 4 + k] = units.astype(BF)
+    ring_take(late, 2)
+    for key, copy in shares.items():
+        if key[0] in late:
+            copy.wait_recv()
     total = normed.astype(F32)
     for k in range(8):
         w = w_down[k // 2, k % 2].reshape(512, 1024)
@@ -451,6 +493,8 @@
     def _():
         pltpu.make_async_copy(attended, attended, mix_send).wait()
 
+    for ring in [*rings.values(), *three]:
+        pending += ring.copies.values()
     for copy in swaps + pending:
         copy.wait_send()
     for copy in keeps:
@@ -461,13 +505,14 @@
 
 
 def layer(x, lengths, w_qkv, w_attn_out, w_in, w_down, ln_gain, ln_bias):
-    vmem, hbm = pl.BlockSpec(memory_space=pltpu.VMEM), pl.BlockSpec(memory_space=pl.ANY)
+    vmem, free = pl.BlockSpec(memory_space=pltpu.VMEM), pl.BlockSpec(memory_space=pl.ANY)
+    hbm = pl.BlockSpec(memory_space=pltpu.HBM)
     dma = pltpu.SemaphoreType.DMA
     return pl.pallas_call(
         layer_kernel,
         out_shape=(jax.ShapeDtypeStruct((12, 64, 256), BF),) * 3,
         in_specs=[hbm, pl.BlockSpec(memory_space=pltpu.SMEM), hbm, hbm, hbm, hbm, vmem, vmem],
-        out_specs=(hbm,) * 3,
+        out_specs=(free,) * 3,
         scratch_shapes=[
             pltpu.VMEM((12, 64, 1024), BF),
             pltpu.VMEM((8, 3072), F32),
@@ -500,18 +545,18 @@
             dma((3,)),
             dma((2, 3)),
             dma((2, 3)),
-            dma((2, 3)),
-            dma((2, 3)),
+            dma((2, 2, 3)),
+            dma((2, 2, 3)),
             dma,
             dma,
             dma,
             dma((2,)),
-            dma((5, 2, 3)),
-            dma((5, 2, 3)),
-            dma((5, 2, 3)),
-            dma((5, 2, 3)),
-            dma((5, 7)),
-            dma((5, 7)),
+            dma((7, 3)),
+            dma((7, 3)),
+            dma((7, 2, 2, 3)),
+            dma((7, 2, 2, 3)),
+            dma((7, 7)),
+            dma((7, 7)),
             dma,
             dma,
             dma,

time: 114 us -> 107 us (0.939)
  the two profiles are of different devices: /device:TPU:1 before, /device:TPU:101 now
where the time goes in v3:
time: 107 us
  Pallas kernels  102 us (95%)
  local copies, waits for them, and re-layouts  4.33 us (4%)
    pallas_call x1, Pallas kernels, layer(): pl.pallas_call(layer_kernel, out_shape=(jax.ShapeDtypeStruct((12, 64, 256...  102 us
    unnamed x5, local copies, waits for them, and re-layouts  4.33 us

profile of v3, /device:TPU:101, one launch (start us, length us, event | category | flops | bytes accessed | tf_op | source)
XLA Modules:
  0.0 106.9 jit_solution(17700590470869658736)
XLA Ops:
  0.6 101.9 %shard_map.103 = (bf16[12,64,256]{2,1,0:T(8,128)(2,1)}, bf16[12,64,256]{2,1,0:T(8,128)(2,1)}, bf16[12,64,256]{2,1,0:T(8,128)(2,1)}) custom-call(bf16[12,64,1024]{2,1,0:T(8,128)(2,1)} %x_hbm.1, s32[12]{0:T(128)} %len_ref.1, f32[8,3072]{1,0:T(8,128)} %qkv_hbm.1, f32[8,1024]{1,0:T(8,128)} %out_hbm.1, f32[8,4096]{1,0:T(8,128)} %in_hbm.1, f32[32,1024]{1,0:T(8,128)} %down_hbm.1, ...), custom_call_target="tpu_custom_call" | custom-call | tf_op jit(solution)/shard_map/pallas_call | solution.py:511
  102.5 0.0 copy-start
  102.5 1.8 %copy.14 = bf16[12,64,256]{2,1,0:T(8,128)(2,1)} copy(bf16[12,64,256]{2,1,0:T(8,128)(2,1)} %get-tuple-element.6) | data formatting | bytes 786432
  104.3 1.8 %copy.15 = bf16[12,64,256]{2,1,0:T(8,128)(2,1)} copy(bf16[12,64,256]{2,1,0:T(8,128)(2,1)} %get-tuple-element.7) | data formatting | bytes 786432
  106.1 0.0 copy-done
  106.1 0.7 copy.16
Async XLA Ops:
  102.5 3.6 %copy-start = (bf16[12,64,256]{2,1,0:T(8,128)(2,1)S(1)}, bf16[12,64,256]{2,1,0:T(8,128)(2,1)}, u32[]{:S(2)}) copy-start(bf16[12,64,256]{2,1,0:T(8,128)(2,1)} %get-tuple-element.8) | copy-start | bytes 1179652

commit v4 on v3

--- a/solution.py
+++ b/solution.py
@@ -14,7 +14,7 @@
 SCORE_FACTOR = 64 ** (-0.5) * math.log2(math.e)
 DEAD = -1e30
 IN_X, IN_Z = 384, 768
-DOWN_X, DOWN_Z = 512, 256
+DOWN_X, DOWN_Z = 384, 384
 
 
 class Place:
@@ -42,9 +42,9 @@
         return (self.s, self.xh * 2 + 1 - self.c)
 
 
-def duty(s):
+def duty(s, h):
     z, xl, y = s // 8, lax.rem(s // 4, 2), lax.rem(s, 4)
-    r = lax.rem(y + z, 4)
+    r = lax.rem(y + z + 2 * lax.rem(h, 2), 4)
     return z * 3 + r, xl, r < 3
 
 
@@ -95,7 +95,7 @@
     share_send, share_recv, mix_send, mix_recv, mix_own, back_send, back_recv, back_own,
 ):
     me = Place()
-    prompt, pair, busy = duty(me.s)
+    prompt, pair, busy = duty(me.s, me.h)
     sibling = me.sibling()
     loads = [
         pltpu.make_async_copy(source, target, load_sem.at[n])
@@ -330,7 +330,7 @@
 
     def post(i, carry):
         to = lax.rem(me.s + i, 32)
-        their_prompt, their_pair, their_busy = duty(to)
+        their_prompt, their_pair, their_busy = duty(to, me.h)
 
         @pl.when(their_busy)
         def _():
@@ -564,12 +564,29 @@
             dma((3,)),
             dma,
         ],
-        compiler_params=pltpu.CompilerParams(collective_id=0, has_side_effects=True, vmem_limit_bytes=58 << 20),
+        compiler_params=pltpu.CompilerParams(collective_id=0, has_side_effects=True, vmem_limit_bytes=46 << 20),
     )(x, lengths, w_qkv, w_attn_out, w_in, w_down, ln_gain, ln_bias)
 
 
+def hand_over(*refs):
+    copies = [pltpu.make_async_copy(refs[n], refs[3 + n], refs[6].at[n]) for n in range(3)]
+    for copy in copies:
+        copy.start()
+    for copy in copies:
+        copy.wait()
+
+
 def per_device(hidden_in, lengths, w_qkv, w_attn_out, w_in, w_down, ln_gain, ln_bias):
-    return layer(hidden_in, lengths, w_qkv, w_attn_out, w_in, w_down, ln_gain, ln_bias)
+    operands = (hidden_in, lengths, w_qkv, w_attn_out, w_in, w_down, ln_gain, ln_bias)
+    made = layer(*(pltpu.with_memory_space_constraint(a, pltpu.HBM) for a in operands))
+    return pl.pallas_call(
+        hand_over,
+        out_shape=tuple(jax.ShapeDtypeStruct(part.shape, part.dtype) for part in made),
+        in_specs=[pl.BlockSpec(memory_space=pl.ANY)] * 3,
+        out_specs=(pl.BlockSpec(memory_space=pltpu.HBM),) * 3,
+        scratch_shapes=[pltpu.SemaphoreType.DMA((3,))],
+        compiler_params=pltpu.CompilerParams(vmem_limit_bytes=1 << 20),
+    )(*made)
 
 
 def solution(mesh):

time: 107 us -> 101 us (0.944)
  the two profiles are of different devices: /device:TPU:101 before, /device:TPU:1 now
where the time goes in v4:
time: 101 us
  Pallas kernels  99.7 us (99%)
    pallas_call x1, Pallas kernels, layer(): pl.pallas_call(layer_kernel, out_shape=(jax.ShapeDtypeStruct((12, 64, 256...  98.7 us

profile of v4, /device:TPU:1, one launch (start us, length us, event | category | flops | bytes accessed | tf_op | source)
XLA Modules:
  0.0 100.5 jit_solution(4115083666617273282)
XLA Ops:
  0.6 98.7 %shard_map.103 = (bf16[12,64,256]{2,1,0:T(8,128)(2,1)S(1)}, bf16[12,64,256]{2,1,0:T(8,128)(2,1)S(1)}, bf16[12,64,256]{2,1,0:T(8,128)(2,1)S(1)}) custom-call(bf16[12,64,1024]{2,1,0:T(8,128)(2,1)} %x_hbm.1, s32[12]{0:T(128)} %len_ref.1, f32[8,3072]{1,0:T(8,128)} %qkv_hbm.1, f32[8,1024]{1,0:T(8,128)} %out_hbm.1, f32[8,4096]{1,0:T(8,128)} %in_hbm.1, ...), custom_call_target="tpu_custom_call" | custom-call | tf_op jit(solution)/shard_map/pallas_call | solution.py:511
  99.3 1.0 %shard_map.104 = (bf16[12,64,256]{2,1,0:T(8,128)(2,1)}, bf16[12,64,256]{2,1,0:T(8,128)(2,1)}, bf16[12,64,256]{2,1,0:T(8,128)(2,1)}) custom-call(bf16[12,64,256]{2,1,0:T(8,128)(2,1)S(1)} %get-tuple-element.6.refs_0_, bf16[12,64,256]{2,1,0:T(8,128)(2,1)S(1)} %get-tuple-element.7.refs_1_, bf16[12,64,256]{2,1,0:T(8,128)(2,1)S(1)} %get-tuple-element.8.refs_2_), custom_call_target="tpu_custom_call" | custom-call | tf_op jit(solution)/shard_map/pallas_call | solution.py:582

commit v5 on v4

--- a/solution.py
+++ b/solution.py
@@ -137,42 +137,18 @@
             in_half, swap_send.at[2], swap_recv.at[2], sibling,
         ),
     ]
+    loads[3].wait()
+    w_down[me.z, me.xl, me.y, me.xh, me.c] = down_f32[...].astype(BF)
     pl.semaphore_wait(barrier, 34)
     for copy in swaps:
         copy.start()
-    loads[3].wait()
-    w_down[me.z, me.xl, me.y, me.xh, me.c] = down_f32[...].astype(BF)
     first = me.c == 0
 
     def stack(mine, sent):
         rows = jnp.concatenate([jnp.where(first, mine, sent), jnp.where(first, sent, mine)], axis=0)
         return rows.astype(BF)
 
-    swaps[0].wait_recv()
-    for k in range(2):
-        for t in range(3):
-            at = pl.multiple_of(t * 1024 + (2 * k + me.c) * 256, 256)
-            cols = slice(k * 768 + t * 256, k * 768 + (t + 1) * 256)
-            slab[k, :, t * 256 : (t + 1) * 256] = stack(qkv_f32[:, pl.ds(at, 256)], qkv_half[:, cols])
-    w_qkv[me.z, me.xl, me.y, me.xh] = slab[me.xh]
     pending = []
-    one = []
-    for d in (1, 3, 2):
-        target = me.peer("x", d)
-        copy = remote(
-            slab.at[target[1] // 2], w_qkv.at[me.z, me.xl, me.y, me.xh], one_send.at[d - 1], one_recv.at[d - 1], target
-        )
-        copy.start()
-        one.append(copy)
-    pending += one
-
-    for n, (source, half, width, target) in enumerate(
-        ((out_f32, out_half, 512, w_out), (in_f32, in_half, 2048, w_in))
-    ):
-        swaps[n + 1].wait_recv()
-        mine = source[:, pl.ds(pl.multiple_of(me.c * width, width), width)]
-        target[me.c, me.z, me.xl, me.y, me.xh] = stack(mine, half[...])
-
     one_c = pl.ds(me.c, 1)
 
     def region(piece, zs, xls, ys, xhs):
@@ -212,9 +188,9 @@
                 xls = pl.ds(half, 1)
         return region(piece, zs, xls, ys, xhs)
 
-    def send_first():
+    def send_first(group):
         started = []
-        for piece in pieces:
+        for piece in group:
             part = area(piece, "")
             for d in (1, 3, 2):
                 copy = remote(
@@ -224,6 +200,31 @@
                 started.append(copy)
                 pending.append(copy)
         return started
+
+    late_one = send_first(late)
+    swaps[0].wait_recv()
+    for k in range(2):
+        for t in range(3):
+            at = pl.multiple_of(t * 1024 + (2 * k + me.c) * 256, 256)
+            cols = slice(k * 768 + t * 256, k * 768 + (t + 1) * 256)
+            slab[k, :, t * 256 : (t + 1) * 256] = stack(qkv_f32[:, pl.ds(at, 256)], qkv_half[:, cols])
+    w_qkv[me.z, me.xl, me.y, me.xh] = slab[me.xh]
+    one = []
+    for d in (1, 3, 2):
+        target = me.peer("x", d)
+        copy = remote(
+            slab.at[target[1] // 2], w_qkv.at[me.z, me.xl, me.y, me.xh], one_send.at[d - 1], one_recv.at[d - 1], target
+        )
+        copy.start()
+        one.append(copy)
+    pending += one
+
+    for n, (source, half, width, target) in enumerate(
+        ((out_f32, out_half, 512, w_out), (in_f32, in_half, 2048, w_in))
+    ):
+        swaps[n + 1].wait_recv()
+        mine = source[:, pl.ds(pl.multiple_of(me.c * width, width), width)]
+        target[me.c, me.z, me.xl, me.y, me.xh] = stack(mine, half[...])
 
     shares = {}
 
@@ -267,7 +268,12 @@
             for way in range(2):
                 share(piece, 1 + way * 3 + step, ring.came(way, step))
 
-    bulk_one = send_first()
+    bulk_one = send_first(early)
+    middle = [rings[piece, 1] for piece in late]
+    for copy in late_one:
+        copy.wait_recv()
+    start(middle, 0)
+    start(middle, 1)
     for copy in one:
         copy.wait_recv()
     left, right = pl.ds(0, 384), pl.ds(384, 384)
@@ -283,9 +289,10 @@
     pending += two
     for copy in bulk_one:
         copy.wait_recv()
-    middle = [rings[piece, 1] for piece in pieces]
+    middle = [rings[piece, 1] for piece in early]
     start(middle, 0)
     start(middle, 1)
+    middle = [rings[piece, 1] for piece in pieces]
     for copy in two:
         copy.wait_recv()
 

time: 101 us -> 98.5 us (0.975)
  Pallas kernels: 99.7 us -> 97.5 us
    pallas_call x1, Pallas kernels: 98.7 us -> 96.4 us  [layer(): pl.pallas_call(layer_kernel, out_shape=(jax.ShapeDtypeStruct((12, 64, 256...]
where the time goes in v5:
time: 98.5 us; the launch traced here: 98.3 us
  Pallas kernels  97.5 us (99%)
    pallas_call x1, Pallas kernels, layer(): pl.pallas_call(layer_kernel, out_shape=(jax.ShapeDtypeStruct((12, 64, 256...  96.4 us

profile of v5, /device:TPU:1, one launch (start us, length us, event | category | flops | bytes accessed | tf_op | source)
XLA Modules:
  0.0 98.3 jit_solution(14913379139746052844)
XLA Ops:
  0.6 96.4 %shard_map.103 = (bf16[12,64,256]{2,1,0:T(8,128)(2,1)S(1)}, bf16[12,64,256]{2,1,0:T(8,128)(2,1)S(1)}, bf16[12,64,256]{2,1,0:T(8,128)(2,1)S(1)}) custom-call(bf16[12,64,1024]{2,1,0:T(8,128)(2,1)} %x_hbm.1, s32[12]{0:T(128)} %len_ref.1, f32[8,3072]{1,0:T(8,128)} %qkv_hbm.1, f32[8,1024]{1,0:T(8,128)} %out_hbm.1, f32[8,4096]{1,0:T(8,128)} %in_hbm.1, ...), custom_call_target="tpu_custom_call" | custom-call | tf_op jit(solution)/shard_map/pallas_call | solution.py:518
  97.1 1.0 %shard_map.104 = (bf16[12,64,256]{2,1,0:T(8,128)(2,1)}, bf16[12,64,256]{2,1,0:T(8,128)(2,1)}, bf16[12,64,256]{2,1,0:T(8,128)(2,1)}) custom-call(bf16[12,64,256]{2,1,0:T(8,128)(2,1)S(1)} %get-tuple-element.6.refs_0_, bf16[12,64,256]{2,1,0:T(8,128)(2,1)S(1)} %get-tuple-element.7.refs_1_, bf16[12,64,256]{2,1,0:T(8,128)(2,1)S(1)} %get-tuple-element.8.refs_2_), custom_call_target="tpu_custom_call" | custom-call | tf_op jit(solution)/shard_map/pallas_call | solution.py:589

commit v6 on v5

--- a/solution.py
+++ b/solution.py
@@ -13,7 +13,7 @@
 EPSILON = 1e-05
 SCORE_FACTOR = 64 ** (-0.5) * math.log2(math.e)
 DEAD = -1e30
-IN_X, IN_Z = 384, 768
+IN_X, IN_Z = 512, 640
 DOWN_X, DOWN_Z = 384, 384
 
 
@@ -105,7 +105,7 @@
             )
         )
     ]
-    for copy in loads:
+    for copy in loads[:4]:
         copy.start()
     barrier = pltpu.get_barrier_semaphore()
 
@@ -138,6 +138,7 @@
         ),
     ]
     loads[3].wait()
+    loads[4].start()
     w_down[me.z, me.xl, me.y, me.xh, me.c] = down_f32[...].astype(BF)
     pl.semaphore_wait(barrier, 34)
     for copy in swaps:
@@ -427,9 +428,9 @@
 
     attend(0, 2)
     ring_take(early, 2)
-    attend(2, 6)
+    attend(2, 7)
     ring_take(late, 0)
-    attend(6, 8)
+    attend(7, 8)
     ring_take(late, 1)
     mine_too = jnp.logical_and(busy, lands_here)
 

time: 98.5 us -> 98 us (level); the launches traced: 98.3 us -> 96.5 us
  Pallas kernels: 97.5 us -> 95.7 us
    pallas_call x1, Pallas kernels: 96.4 us -> 94.7 us  [layer(): pl.pallas_call(layer_kernel, out_shape=(jax.ShapeDtypeStruct((12, 64, 256...]
where the time goes in v6:
time: 98 us; the launch traced here: 96.5 us
  Pallas kernels  95.7 us (98%)
    pallas_call x1, Pallas kernels, layer(): pl.pallas_call(layer_kernel, out_shape=(jax.ShapeDtypeStruct((12, 64, 256...  94.7 us

profile of v6, /device:TPU:1, one launch (start us, length us, event | category | flops | bytes accessed | tf_op | source)
XLA Modules:
  0.0 96.5 jit_solution(11330609791431457219)
XLA Ops:
  0.6 94.7 %shard_map.103 = (bf16[12,64,256]{2,1,0:T(8,128)(2,1)S(1)}, bf16[12,64,256]{2,1,0:T(8,128)(2,1)S(1)}, bf16[12,64,256]{2,1,0:T(8,128)(2,1)S(1)}) custom-call(bf16[12,64,1024]{2,1,0:T(8,128)(2,1)} %x_hbm.1, s32[12]{0:T(128)} %len_ref.1, f32[8,3072]{1,0:T(8,128)} %qkv_hbm.1, f32[8,1024]{1,0:T(8,128)} %out_hbm.1, f32[8,4096]{1,0:T(8,128)} %in_hbm.1, ...), custom_call_target="tpu_custom_call" | custom-call | tf_op jit(solution)/shard_map/pallas_call | solution.py:519
  95.3 1.0 %shard_map.104 = (bf16[12,64,256]{2,1,0:T(8,128)(2,1)}, bf16[12,64,256]{2,1,0:T(8,128)(2,1)}, bf16[12,64,256]{2,1,0:T(8,128)(2,1)}) custom-call(bf16[12,64,256]{2,1,0:T(8,128)(2,1)S(1)} %get-tuple-element.6.refs_0_, bf16[12,64,256]{2,1,0:T(8,128)(2,1)S(1)} %get-tuple-element.7.refs_1_, bf16[12,64,256]{2,1,0:T(8,128)(2,1)S(1)} %get-tuple-element.8.refs_2_), custom_call_target="tpu_custom_call" | custom-call | tf_op jit(solution)/shard_map/pallas_call | solution.py:590

commit v7 on v6

--- a/solution.py
+++ b/solution.py
@@ -167,7 +167,7 @@
     }
     order = {0: "yzx", 1: "yzx", 2: "xyz", 3: "zxy", 4: "yzx", 5: "xyz", 6: "zxy"}
     early, late = (0, 1, 2, 3), (4, 5, 6)
-    pieces = early + late
+    pieces = late + early
 
     def area(piece, done, at=None, half=None):
         x, y, z = me.x, me.y, me.z
@@ -476,7 +476,7 @@
     own = pltpu.make_async_copy(result.at[me.h], hidden_hbm.at[rows], back_own)
     own.start()
     last = []
-    for d in range(1, 4):
+    for d in (2, 3, 1):
         to = lax.rem(me.h + d, 4)
         copy = remote(result.at[to], hidden_hbm.at[rows], back_send.at[d - 1], back_recv.at[d - 1], (me.s, to))
         copy.start()

time: 98 us -> 98 us (level)
  no operation moved by 1% of the time
where the time goes in v7:
time: 98 us; the launch traced here: 96.7 us
  Pallas kernels  95.9 us (98%)
    pallas_call x1, Pallas kernels, layer(): pl.pallas_call(layer_kernel, out_shape=(jax.ShapeDtypeStruct((12, 64, 256...  94.9 us

profile of v7, /device:TPU:1, one launch (start us, length us, event | category | flops | bytes accessed | tf_op | source)
XLA Modules:
  0.0 96.7 jit_solution(12304033126089919933)
XLA Ops:
  0.6 94.9 %shard_map.103 = (bf16[12,64,256]{2,1,0:T(8,128)(2,1)S(1)}, bf16[12,64,256]{2,1,0:T(8,128)(2,1)S(1)}, bf16[12,64,256]{2,1,0:T(8,128)(2,1)S(1)}) custom-call(bf16[12,64,1024]{2,1,0:T(8,128)(2,1)} %x_hbm.1, s32[12]{0:T(128)} %len_ref.1, f32[8,3072]{1,0:T(8,128)} %qkv_hbm.1, f32[8,1024]{1,0:T(8,128)} %out_hbm.1, f32[8,4096]{1,0:T(8,128)} %in_hbm.1, ...), custom_call_target="tpu_custom_call" | custom-call | tf_op jit(solution)/shard_map/pallas_call | solution.py:519
  95.5 1.0 %shard_map.104 = (bf16[12,64,256]{2,1,0:T(8,128)(2,1)}, bf16[12,64,256]{2,1,0:T(8,128)(2,1)}, bf16[12,64,256]{2,1,0:T(8,128)(2,1)}) custom-call(bf16[12,64,256]{2,1,0:T(8,128)(2,1)S(1)} %get-tuple-element.6.refs_0_, bf16[12,64,256]{2,1,0:T(8,128)(2,1)S(1)} %get-tuple-element.7.refs_1_, bf16[12,64,256]{2,1,0:T(8,128)(2,1)S(1)} %get-tuple-element.8.refs_2_), custom_call_target="tpu_custom_call" | custom-call | tf_op jit(solution)/shard_map/pallas_call | solution.py:590
